TPU v7x, 32 devices: a whole 2x2x4 slice. The times are simulated.
32 devices in a mesh: site: 8 (over z, x), task: 4 (over y, core).
Axes of the slice: x: 2, y: 2, z: 4, core: 2. Of those that a mesh axis runs over, the one named last changes fastest.
Arguments:
- values: bfloat16 [1024, 65536], P('task', 'site'), may hold values from -6 to 6
- factors: bfloat16 [1024, 128], P('task'), may hold values from -0.1875 to 0.1875
- jitter: bfloat16 [2, 65536], P(None, 'site'), may hold values from 0 to 1
- length_scales: float32 [4], replicated, may hold values from 1.1 to 2.5
- nugget: float32 [1024], P('task'), may hold values from 0.1 to 1
- neighbours: int32 [256, 3], P('site'), may hold values from -1 to 255, as said below
Outputs:
- product: float32 [1024, 65536], P('task', 'site')
Inputs may be any that keep to these rules, and one draw needn't show every extreme that they name: `neighbours`: row a is (a, (a - 1) mod 256, (a + 1) mod 256), where an entry is -1 if a barrier separates the two tiles; a barrier between tiles a and (a + 1) mod 256 removes each from the other's row.
All inputs are finite; a program needn't handle non-finite values.
Results may differ from a plain program's by a relative error of at most 0.0034.
Values may be sent and summed in bfloat16 or wider, within the bound.
No kernel may reach another device: no remote copies, remote signals or barrier semaphores. Data moves between devices by JAX's collectives and lax.ppermute only.
A program may use at most 64 MiB of HBM per device.

v0:
```python
import jax
import jax.numpy as jnp
from jax import lax
from jax.sharding import PartitionSpec as P

R = 32
SIDE = 16
TILE = 256
HALO_TILES = 1


def padded(array, sides, width):
    for axis, dim in sides:
        peers, length = (lax.axis_size(axis), array.shape[dim])
        up = [(i, (i + 1) % peers) for i in range(peers)]
        down = [(j, i) for i, j in up]
        last = lax.slice_in_dim(array, length - width, length, axis=dim)
        initial = lax.slice_in_dim(array, 0, width, axis=dim)
        before = lax.ppermute(last, axis, up)
        after = lax.ppermute(initial, axis, down)
        array = jnp.concatenate([before, array, after], axis=dim)
    return array


def make_kernel(tile_shift, present, own_jitter, far_jitter, scales):
    positions = jnp.arange(TILE, dtype=jnp.int32)
    grid_rows = (positions // SIDE).astype(jnp.float32)
    grid_cols = (positions % SIDE).astype(jnp.float32)
    far_across = far_jitter[0].astype(jnp.float32) + grid_rows
    far_side = far_jitter[1].astype(jnp.float32) + grid_cols
    own_across = own_jitter[0].astype(jnp.float32) + grid_rows
    own_side = own_jitter[1].astype(jnp.float32) + grid_cols
    across = (
        (tile_shift * SIDE).astype(jnp.float32)[:, :, None, None]
        + far_across[:, :, None, :]
        - own_across[:, None, :, None]
    )
    sideways = far_side[:, :, None, :] - own_side[:, None, :, None]
    distance = across * across + sideways * sideways
    scaled = distance[None] / (scales * scales)[:, None, None, None, None]
    inside = jnp.maximum(1.0 - scaled, 0.0)
    weight = inside * inside * inside * (1.0 + 3.0 * scaled) * present[None, :, :, None, None]
    return weight.astype(jnp.bfloat16)


def apply_kernels(wide_proj, wide_jitter, neighbours, scales, groups):
    row_count = wide_proj.shape[0]
    extent = wide_proj.shape[1] // TILE
    tiles_dev = neighbours.shape[0]
    total_tiles = tiles_dev * lax.axis_size("site")
    own_ids = lax.axis_index("site") * tiles_dev + jnp.arange(tiles_dev, dtype=jnp.int32)
    valid = neighbours >= 0
    safe_ids = jnp.where(valid, neighbours, own_ids[:, None])
    present_all = valid.astype(jnp.float32)
    tile_shift = (safe_ids - own_ids[:, None] + total_tiles // 2) % total_tiles - total_tiles // 2
    tile_slot = jnp.arange(tiles_dev, dtype=jnp.int32)[:, None] + HALO_TILES + tile_shift
    proj_tiles = wide_proj.reshape(groups, row_count // groups, extent, TILE)
    jitter_tiles = wide_jitter.reshape(2, extent, TILE)
    own_all = jitter_tiles[:, HALO_TILES : HALO_TILES + tiles_dev]

    def advance(pair_index):
        begin = pair_index * 2
        slots = lax.dynamic_slice_in_dim(tile_slot, begin, 2, 0)
        shifts = lax.dynamic_slice_in_dim(tile_shift, begin, 2, 0)
        present = lax.dynamic_slice_in_dim(present_all, begin, 2, 0)
        own_jitter = lax.dynamic_slice_in_dim(own_all, begin, 2, 1)
        far_jitter = jnp.take(jitter_tiles, slots, axis=1)
        kernel = make_kernel(shifts, present, own_jitter, far_jitter, scales)
        pieces = jnp.take(proj_tiles, slots, axis=2)
        return jnp.einsum("gbkij,grbkj->grbi", kernel, pieces, preferred_element_type=jnp.float32)

    blocks = lax.map(advance, jnp.arange(tiles_dev // 2, dtype=jnp.int32))
    return blocks.transpose(1, 2, 0, 3, 4).reshape(row_count, tiles_dev * TILE)


def per_device(values, factors, jitter, length_scales, nugget, neighbours):
    partial_sum = lax.dot_general(
        factors, values, (((0,), (0,)), ((), ())), preferred_element_type=jnp.float32
    )
    projected = lax.psum_scatter(partial_sum, "task", scatter_dimension=0, tiled=True).astype(
        jnp.bfloat16
    )
    latent_id = lax.axis_index("task") * projected.shape[0] // R
    scales = lax.dynamic_slice_in_dim(length_scales, latent_id, 1)
    groups = 1
    stacked = jnp.concatenate([projected, jitter], axis=0)
    widened = padded(stacked, (("site", 1),), HALO_TILES * TILE)
    smoothed = apply_kernels(widened[:-2], widened[-2:], neighbours, scales, groups).astype(
        jnp.bfloat16
    )
    own_term = nugget[:, None] * values.astype(jnp.float32)
    mixed = jnp.dot(
        factors,
        lax.all_gather(smoothed, "task", axis=0, tiled=True),
        preferred_element_type=jnp.float32,
    )
    return mixed + own_term


def solution(mesh):
    return jax.shard_map(
        per_device,
        mesh=mesh,
        in_specs=(
            P("task", "site"),
            P("task", None),
            P(None, "site"),
            P(),
            P("task"),
            P("site", None),
        ),
        out_specs=P("task", "site"),
        check_vma=False,
    )
```

profile of v0, /device:TPU:0, one launch (start us, length us, event | category | flops | bytes accessed | tf_op | source)
XLA Modules:
  0.0 180.5 jit_solution(7709852470511888179)
XLA Ops:
  7.4 4.9 %fusion.35 = f32[128,8192]{1,0:T(8,128)} fusion(bf16[256,128]{1,0:T(8,128)(2,1)S(1)} %copy-done, bf16[256,8192]{1,0:T(8,128)(2,1)} %param.8), kind=kOutput, calls=%fused_computation.72 | convolution fusion | flops 536870912 | bytes 8454144 | tf_op jit(solution)/shard_map/dot_general | solution.py:77
  13.2 46.6 %reduce-scatter.2.cloned.1.call-done = f32[32,8192]{1,0:T(8,128)} async-done(((f32[128,8192]{1,0:T(8,128)}), f32[32,8192]{1,0:T(8,128)}) %reduce-scatter.2.cloned.1.call-update) | async-done | bytes 1048592 | tf_op jit(solution)/shard_map/reduce_scatter | solution.py:80
  59.8 1.3 convert_element_type.123
  61.1 1.5 collective-permute-start
  62.6 3.2 %collective-permute-start.1 = (bf16[34,256]{1,0:T(8,128)(2,1)S(1)}, bf16[34,256]{1,0:T(8,128)(2,1)S(1)}, u32[]{:S(2)}, u32[]{:S(2)}) collective-permute-start(bf16[34,256]{1,0:T(8,128)(2,1)S(1)} %get-tuple-element.197), channel_id=1, source_target_pairs={{4,0},{8,4},{12,8},{16,12},{20,16},{24,20},{28,24},{0,28},{5,1},{9... | collective-permute-start | bytes 52232 | tf_op jit(solution)/shard_map/ppermute | solution.py:20
  68.6 64.2 %while.12 = (s32[]{:T(128)}, bf16[16,1,32,2,256]{4,2,3,1,0:T(8,128)(2,1)S(1)}, s32[16]{0:T(128)S(1)}, s32[32,3]{1,0:T(8,128)S(1)}, bf16[1,32,34,256]{3,1,2,0:T(8...) while((s32[]{:T(128)}, ...), condition=%wide.region_2.3_spmd, body=%wide.region_1.2_spmd.sunk | while | flops 31130680 | bytes 467087 | solution.py:72
  71.6 1.0 fusion.51
  75.6 1.0 fusion.51
  79.6 1.0 fusion.51
  87.7 1.0 fusion.51
  91.7 1.0 fusion.51
  95.7 1.0 fusion.51
  103.7 1.0 fusion.51
  107.7 1.0 fusion.51
  111.7 1.0 fusion.51
  119.8 1.0 fusion.51
  123.8 1.0 fusion.51
  127.8 1.0 fusion.51
  131.8 1.0 fusion.51
  133.3 1.2 convert_element_type.127
  134.6 6.4 %copy.41 = bf16[256,8192]{0,1:T(8,128)(2,1)} copy(bf16[256,8192]{1,0:T(8,128)(2,1)} %param.8) | data formatting | bytes 8388608 | tf_op args[0]
  140.9 16.5 %all-gather.2.cloned.1.call-done = bf16[128,8192]{1,0:T(8,128)(2,1)} async-done(((bf16[32,8192]{1,0:T(8,128)(2,1)}), bf16[128,8192]{1,0:T(8,128)(2,1)}) %all-gather.2.cloned.1.call-update) | async-done | bytes 2097168 | tf_op jit(solution)/shard_map/all_gather | solution.py:94
  157.4 7.3 %fusion.29 = f32[256,8192]{0,1:T(8,128)} fusion(bf16[128,8192]{1,0:T(8,128)(2,1)} %all-gather.2.cloned.1.call-done, bf16[256,128]{1,0:T(8,128)(2,1)S(1)} %copy-done, bf16[256,8192]{0,1:T(8,128)(2,1)} %copy.41, f32[256]{0:T(256)S(1)} %copy-done.2), kind=kOutput, calls=%fused_computation.54 | convolution fusion | flops 543162368 | bytes 14746624 | tf_op jit(solution)/shard_map/dot_general | solution.py:92
  164.8 8.9 %copy.42 = f32[256,8192]{1,0:T(8,128)} copy(f32[256,8192]{0,1:T(8,128)} %fusion.29) | data formatting | bytes 16777216 | tf_op jit(solution)/shard_map/add | solution.py:97
  (307 shorter events, 43.1 us)
Async XLA Ops:
  6.5 0.8 copy-start
  6.5 53.3 %reduce-scatter.2.cloned.1.call-start = ((), (), s32[]{:S(2)}) async-start(), calls=%async_computation.1 | async-start | bytes 5242880 | tf_op jit(solution)/shard_map/reduce_scatter | solution.py:80
  12.3 0.7 copy-start.3
  12.3 48.7 %copy-start.1 = (bf16[2,8192]{1,0:T(2,128)(2,1)S(1)}, bf16[2,8192]{1,0:T(2,128)(2,1)}, u32[]{:S(2)}) copy-start(bf16[2,8192]{1,0:T(2,128)(2,1)} %param.10) | copy-start | bytes 98308
  12.4 53.5 %copy-start.4 = (f32[4]{0:T(128)S(1)}, f32[4]{0:T(128)}, u32[]{:S(2)}) copy-start(f32[4]{0:T(128)} %param.11) | copy-start | bytes 52
  12.4 145.1 %all-gather.2.cloned.1.call-start = ((), (), s32[]{:S(2)}) async-start(), calls=%async_computation.2 | async-start | bytes 2621440 | tf_op jit(solution)/shard_map/all_gather | solution.py:94
  61.1 6.8 %collective-permute-start = (bf16[34,256]{1,0:T(8,128)(2,1)S(1)}, bf16[34,256]{1,0:T(8,128)(2,1)S(1)}, u32[]{:S(2)}, u32[]{:S(2)}) collective-permute-start(bf16[34,256]{1,0:T(8,128)(2,1)S(1)} %get-tuple-element.196), channel_id=1, source_target_pairs={{0,4},{4,8},{8,12},{12,16},{16,20},{20,24},{24,28},{28,0},{1,5},{5... | collective-permute-start | bytes 52232 | tf_op jit(solution)/shard_map/ppermute | solution.py:19
  62.6 5.3 %collective-permute-start.1 = (bf16[34,256]{1,0:T(8,128)(2,1)S(1)}, bf16[34,256]{1,0:T(8,128)(2,1)S(1)}, u32[]{:S(2)}, u32[]{:S(2)}) collective-permute-start(bf16[34,256]{1,0:T(8,128)(2,1)S(1)} %get-tuple-element.197), channel_id=1, source_target_pairs={{4,0},{8,4},{12,8},{16,12},{20,16},{24,20},{28,24},{0,28},{5,1},{9... | collective-permute-start | bytes 52232 | tf_op jit(solution)/shard_map/ppermute | solution.py:20
  134.5 22.9 %copy-start.2 = (f32[256]{0:T(256)S(1)}, f32[256]{0:T(256)}, u32[]{:S(2)}) copy-start(f32[256]{0:T(256)} %param.12) | copy-start | bytes 3076
Sparse Core Ops, SparseCore 0:
  12.5 47.2 reduce-scatter.1
  134.7 22.7 all-gather.1
where the time goes:
time: 181 us
  waiting for transfers between devices  63.1 us (35%)
  local copies, waits for them, and re-layouts  53.3 us (29%)
  matrix products  27.6 us (15%)
  between operations  14.9 us (8%)
  loops' own time  12.1 us (7%)
  starting transfers between devices  4.82 us (3%)
  other arithmetic  4.62 us (3%)
    reduce_scatter x1, waiting for transfers between devices, per_device(): lax.psum_scatter(partial_sum, 'task', scatter_dimension=0, tiled=True)  46.6 us
    all_gather x1, waiting for transfers between devices, per_device(): lax.all_gather(smoothed, 'task', axis=0, tiled=True)  16.5 us
    dot_general x16, matrix products, advance(): jnp.einsum('gbkij,grbkj->grbi', kernel, pieces, preferred_element_type=jn...  15.3 us
    another operation x1, loops' own time, apply_kernels(): blocks = lax.map(advance, jnp.arange(tiles_dev // 2, dtype=jnp.int32))  12.1 us
    dynamic_slice x16, local copies, waits for them, and re-layouts, apply_kernels(): blocks = lax.map(advance, jnp.arange(tiles_dev // 2, dtype=jnp.int32))  10.6 us
    gather x16, local copies, waits for them, and re-layouts, advance(): far_jitter = jnp.take(jitter_tiles, slots, axis=1)  9.21 us
    add x1, local copies, waits for them, and re-layouts, per_device(): return mixed + own_term  8.89 us
    gather x16, local copies, waits for them, and re-layouts, advance(): pieces = jnp.take(proj_tiles, slots, axis=2)  8.83 us
  transfers between devices with their start and end apart: 4, of which 2 were waited for; matrix products, arithmetic and copies ran while one was open for 4% of the time, Pallas kernels for 0%

commit v1 on v0

v1 whole, which is shorter than its diff:
```python
import jax
import jax.numpy as jnp
from jax import lax
from jax.experimental import pallas as pl
from jax.experimental.pallas import tpu as pltpu
from jax.sharding import PartitionSpec as P

SIDE = 16
TILE = 256
GROUP = 128
HALF = GROUP // 2
REACH = 3 * SIDE
KAPPA = 3.0**-0.25
FAR_AWAY = 1024.0
STEP = 512
EDGE_ROWS = 16
MIB = 1 << 20

VM = pl.BlockSpec(memory_space=pltpu.VMEM)
SM = pl.BlockSpec(memory_space=pltpu.SMEM)
ANY = pl.BlockSpec(memory_space=pl.ANY)


def shape(dims, kind):
    return jax.ShapeDtypeStruct(dims, kind)


def grant(mib):
    return pltpu.CompilerParams(vmem_limit_bytes=mib * MIB)


def cost(flops, size):
    return pl.CostEstimate(flops=flops, bytes_accessed=size, transcendentals=0)


def project(values, factors, core):
    tasks, ranks = factors.shape
    half, width = ranks // 2, values.shape[1]
    steps = width // STEP

    def body(core_ref, f_ref, v_hbm, own_ref, send_ref, v_buf, p_buf, sems):
        spans = [pl.ds(i * STEP, STEP) for i in range(steps)]
        copies = [pltpu.make_async_copy(v_hbm.at[:, s], v_buf.at[:, s], sems.at[i]) for i, s in enumerate(spans)]
        for copy in copies:
            copy.start()
        mine = pl.multiple_of(core_ref[0] * half, half)
        other = pl.multiple_of((1 - core_ref[0]) * half, half)
        turned = f_ref[...].astype(jnp.float32).T.astype(jnp.bfloat16)
        for copy, s in zip(copies, spans):
            copy.wait()
            p_buf[:, s] = jnp.dot(turned, v_buf[:, s], preferred_element_type=jnp.float32)
            own_ref[:, s] = p_buf[pl.ds(mine, half), s]
            send_ref[:, s] = p_buf[pl.ds(other, half), s].astype(jnp.bfloat16)

    return pl.pallas_call(
        body,
        out_shape=(shape((half, width), jnp.float32), shape((half, width), jnp.bfloat16)),
        in_specs=[SM, VM, ANY],
        out_specs=(VM, VM),
        scratch_shapes=[
            pltpu.VMEM((tasks, width), values.dtype),
            pltpu.VMEM((ranks, width), jnp.float32),
            pltpu.SemaphoreType.DMA((steps,)),
        ],
        compiler_params=grant(14),
        cost_estimate=cost(2 * tasks * ranks * width, tasks * width * 2),
        name="project",
    )(core, factors, values)


def add_cores(own, received, jitter, chunks):
    half, width = own.shape
    edge = half + EDGE_ROWS

    def body(own_ref, got_ref, j_ref, *outs):
        for (begin, end), out in zip(chunks, outs):
            s = slice(begin * GROUP, end * GROUP)
            out[...] = (own_ref[:, s] + got_ref[:, s].astype(jnp.float32)).astype(jnp.bfloat16)
        for out, source, s in (
            (outs[-2], outs[0], slice(0, GROUP)),
            (outs[-1], outs[len(chunks) - 1], slice(-GROUP, None)),
        ):
            out[:half, :] = source[:, s]
            out[half:, :] = jnp.zeros((EDGE_ROWS, GROUP), jnp.bfloat16)
            out[half : half + 2, :] = j_ref[:, s]

    return pl.pallas_call(
        body,
        out_shape=[shape((half, (e - b) * GROUP), jnp.bfloat16) for b, e in chunks] + [shape((edge, GROUP), jnp.bfloat16)] * 2,
        in_specs=[VM, VM, VM],
        out_specs=[VM] * (len(chunks) + 2),
        compiler_params=grant(6),
        cost_estimate=cost(half * width, half * width * 8),
        name="add_cores",
    )(own, received, jitter)


def kernel_blocks(jitter, edges, neighbours, scales, core, region, groups, lat):
    begin, end = region
    near = GROUP + REACH
    far = 2 * GROUP - REACH
    half_rows = edges.shape[0] - EDGE_ROWS if edges is not None else 0

    def body(core_ref, near_ref, scale_ref, j_ref, *rest):
        k_ref = rest[-1]
        lane = lax.broadcasted_iota(jnp.int32, (8, 2 * GROUP), 1)
        sub = lax.broadcasted_iota(jnp.int32, (8, 2 * GROUP), 0)
        position = jnp.where(lane < GROUP + HALF, lane, lane - 2 * GROUP)
        row = (position >> 4).astype(jnp.float32)
        col = (position & (SIDE - 1)).astype(jnp.float32)
        mixed_lane = lax.broadcasted_iota(jnp.int32, (2, GROUP), 1)
        own_lane = lax.broadcasted_iota(jnp.int32, (8, GROUP), 1)
        own_sub = lax.broadcasted_iota(jnp.int32, (8, GROUP), 0)
        own_row = (own_lane >> 4).astype(jnp.float32)
        own_col = (own_lane & (SIDE - 1)).astype(jnp.float32)
        betas = []
        for q in range(lat):
            scale = jnp.full((8, GROUP), scale_ref[core_ref[0] * lat + q], jnp.float32)
            betas.append((1.0 / (KAPPA * scale * scale))[:1])

        def offsets(b):
            return j_ref[:, pl.ds(pl.multiple_of(b * GROUP, GROUP), GROUP)].astype(jnp.float32)

        def block(b, first=False, last=False):
            outside = rest[0][half_rows : half_rows + 2, :].astype(jnp.float32) if first or last else None
            here = offsets(b)
            before = outside if first else offsets(b - 1)
            after = outside if last else offsets(b + 1)
            there = jnp.concatenate([here, jnp.where(mixed_lane < HALF, after, before)], axis=1)
            tile, odd = b // 2, lax.rem(b, 2)
            left_gap = jnp.where((odd == 0) & (near_ref[tile, 1] < 0), FAR_AWAY, 0.0)
            right_gap = jnp.where((odd == 1) & (near_ref[tile, 2] < 0), FAR_AWAY, 0.0)
            gap = jnp.where(lane < GROUP, 0.0, jnp.where(lane < GROUP + HALF, right_gap, left_gap))
            pairs = []
            for axis, base, own_base in ((0, row, own_row), (1, col, own_col)):
                there_8 = jnp.broadcast_to(there[axis : axis + 1], (8, 2 * GROUP))
                here_8 = jnp.broadcast_to(here[axis : axis + 1], (8, GROUP))
                extra = gap if axis == 0 else jnp.zeros_like(gap)
                ones = jnp.where(sub < 5, 1.0, 0.0)
                left = jnp.where(sub == 0, there_8, jnp.where(sub == 1, base, jnp.where(sub == 2, extra, ones)))
                right = jnp.where(own_sub < 3, 1.0, jnp.where(own_sub == 3, -here_8, jnp.where(own_sub == 4, -own_base, 0.0)))
                pairs.append((left.T.astype(jnp.bfloat16), right.astype(jnp.bfloat16)))
            slot = b - begin
            for low, high in ((0, near), (far, 2 * GROUP)):
                across, sideways = (jnp.dot(l[low:high], r, preferred_element_type=jnp.float32) for l, r in pairs)
                distance = across * across + sideways * sideways
                for q in range(lat):
                    u = jnp.maximum(1.0 / KAPPA - betas[q] * distance, 0.0)
                    weight = u * u * u * (4.0 * KAPPA**3 - u)
                    k_ref[slot, low:high, q * GROUP : (q + 1) * GROUP] = weight.astype(jnp.bfloat16)
            k_ref[slot, near:far, :] = jnp.zeros((far - near, lat * GROUP), jnp.bfloat16)

        low, high = begin, end
        if begin == 0:
            block(0, first=True)
            low = 1
        if end == groups:
            block(groups - 1, last=True)
            high = groups - 1
        count = 4
        whole = (high - low) // count

        def several(i, carry):
            for m in range(count):
                block(low + i * count + m)
            return carry

        lax.fori_loop(0, whole, several, 0)
        for b in range(low + whole * count, high):
            block(b)

    size = (end - begin) * 2 * GROUP * lat * GROUP
    args = [core, neighbours, scales, jitter] + ([edges] if edges is not None else [])
    return pl.pallas_call(
        body,
        out_shape=shape((end - begin, 2 * GROUP, lat * GROUP), jnp.bfloat16),
        in_specs=[SM, SM, SM] + [VM] * (len(args) - 3),
        out_specs=VM,
        compiler_params=grant(6),
        cost_estimate=cost(30 * size, 2 * size),
        name="kernel_blocks",
    )(*args)


def smooth(blocks, region, pieces, lat, rank):
    begin, end = region
    half = lat * rank

    def body(k_ref, *refs):
        out = refs[-1]
        first_half = lax.broadcasted_iota(jnp.int32, (1, GROUP), 1) < HALF

        def part(group, which, rows):
            for n, (low, high, _) in enumerate(pieces):
                if low <= group < high:
                    return refs[2 * n + which][rows, (group - low) * GROUP : (group - low + 1) * GROUP]

        for b in range(begin, end):
            for q in range(lat):
                rows = slice(q * rank, (q + 1) * rank)
                sides = [
                    jnp.concatenate(
                        [part(b, w, rows), jnp.where(first_half, part(b + 1, w, rows), part(b - 1, w, rows))], axis=1
                    )
                    for w in range(2)
                ]
                total = jnp.dot(
                    jnp.concatenate(sides, axis=0),
                    k_ref[b - begin, :, q * GROUP : (q + 1) * GROUP],
                    preferred_element_type=jnp.float32,
                )
                out[rows, (b - begin) * GROUP : (b - begin + 1) * GROUP] = (total[:rank] + total[rank:]).astype(jnp.bfloat16)

    arrays = [a for _, _, pair in pieces for a in pair]
    count = (end - begin) * GROUP
    return pl.pallas_call(
        body,
        out_shape=shape((half, count), jnp.bfloat16),
        in_specs=[VM] * (1 + len(arrays)),
        out_specs=VM,
        compiler_params=grant(8),
        cost_estimate=cost(8 * half * GROUP * count, 4 * GROUP * lat * count),
        name="smooth",
    )(blocks, *arrays)


def mix(own, received, factors, nugget, values, product, core, region):
    tasks, ranks = factors.shape
    half = ranks // 2
    first, width = region[0] * GROUP, (region[1] - region[0]) * GROUP
    steps = width // STEP

    def body(core_ref, own_ref, got_ref, f_ref, g_ref, v_hbm, *rest):
        o_hbm, v_buf, o_buf, s_buf, in_sems, out_sems = rest[-6:]
        spans = [pl.ds(i * STEP, STEP) for i in range(steps)]
        places = [pl.ds(first + i * STEP, STEP) for i in range(steps)]
        reads = [pltpu.make_async_copy(v_hbm.at[:, p], v_buf.at[:, s], in_sems.at[i]) for i, (s, p) in enumerate(zip(spans, places))]
        writes = [pltpu.make_async_copy(o_buf.at[:, s], o_hbm.at[:, p], out_sems.at[i]) for i, (s, p) in enumerate(zip(spans, places))]
        for copy in reads:
            copy.start()
        s_buf[pl.ds(pl.multiple_of(core_ref[0] * half, half), half), :] = own_ref[...]
        s_buf[pl.ds(pl.multiple_of((1 - core_ref[0]) * half, half), half), :] = got_ref[...]
        noise = jnp.broadcast_to(g_ref[...], (8, tasks)).T[:, :1]
        for i, s in enumerate(spans):
            reads[i].wait()
            mixed = jnp.dot(f_ref[...], s_buf[:, s], preferred_element_type=jnp.float32)
            o_buf[:, s] = mixed + noise * v_buf[:, s].astype(jnp.float32)
            writes[i].start()
        for copy in writes:
            copy.wait()

    args = [core, own, received, factors, nugget, values]
    specs = [SM, VM, VM, VM, VM, ANY]
    alias = {}
    if product is not None:
        args.append(product)
        specs.append(ANY)
        alias = {6: 0}
    return pl.pallas_call(
        body,
        out_shape=shape(values.shape, jnp.float32),
        in_specs=specs,
        out_specs=ANY,
        scratch_shapes=[
            pltpu.VMEM((tasks, width), values.dtype),
            pltpu.VMEM((tasks, width), jnp.float32),
            pltpu.VMEM((ranks, width), jnp.bfloat16),
            pltpu.SemaphoreType.DMA((steps,)),
            pltpu.SemaphoreType.DMA((steps,)),
        ],
        input_output_aliases=alias,
        compiler_params=grant(10),
        cost_estimate=cost(2 * tasks * ranks * width, tasks * width * 6),
        name="mix",
    )(*args)


def partners(size, bit):
    return [(i, i ^ bit) for i in range(size)]


def sum_fields(share, size):
    bit, other = 2, None
    while bit < size:
        if other is not None:
            share = (share.astype(jnp.float32) + other.astype(jnp.float32)).astype(jnp.bfloat16)
        other = lax.ppermute(share, "task", partners(size, bit))
        bit *= 2
    return share, other


def per_device(values, factors, jitter, length_scales, nugget, neighbours):
    peers, blocks = lax.axis_size("task"), lax.axis_size("site")
    ranks = factors.shape[1]
    lat = length_scales.shape[0] // 2
    rank = ranks // length_scales.shape[0]
    groups = values.shape[1] // GROUP
    core = (lax.axis_index("task") % 2).astype(jnp.int32).reshape(1)
    cuts = [0, groups * 5 // 16, groups * 10 // 16, groups * 14 // 16, groups]
    regions = list(zip(cuts[:-1], cuts[1:]))
    chunk_cuts = [0] + [c + 1 for c in cuts[1:-1]] + [groups]
    chunks = list(zip(chunk_cuts[:-1], chunk_cuts[1:]))

    own, send = project(values, factors, core)
    received = lax.ppermute(send, "task", partners(peers, 1))
    *shares, left_edge, right_edge = add_cores(own, received, jitter, chunks)
    sums = [sum_fields(share, peers) for share in shares]

    up = [(i, (i + 1) % blocks) for i in range(blocks)]
    down = [(j, i) for i, j in up]
    from_left = lax.ppermute(right_edge, "site", up)
    from_right = lax.ppermute(left_edge, "site", down)
    first_half = lax.broadcasted_iota(jnp.int32, from_left.shape, 1) < HALF
    edges = jnp.where(first_half, from_right, from_left)
    edge_sums = sum_fields(edges, peers)

    product = None
    nugget = nugget.reshape(1, -1)
    for n, region in enumerate(regions):
        begin, end = region
        outer = begin == 0 or end == groups
        kernel = kernel_blocks(jitter, edges if outer else None, neighbours, length_scales, core, region, groups, lat)
        pieces = [(*chunks[n], sums[n])]
        if n > 0:
            pieces.append((*chunks[n - 1], sums[n - 1]))
        if begin == 0:
            pieces.append((-1, 0, edge_sums))
        if end == groups:
            pieces.append((groups, groups + 1, edge_sums))
        smoothed = smooth(kernel, region, pieces, lat, rank)
        other = lax.ppermute(smoothed, "task", partners(peers, 1))
        product = mix(smoothed, other, factors, nugget, values, product, core, region)
    return product


def solution(mesh):
    return jax.shard_map(
        per_device,
        mesh=mesh,
        in_specs=(
            P("task", "site"),
            P("task", None),
            P(None, "site"),
            P(),
            P("task"),
            P("site", None),
        ),
        out_specs=P("task", "site"),
        check_vma=False,
    )
```

time: 181 us -> 61.8 us (0.34)
  local copies, waits for them, and re-layouts: 53.3 us -> 3.17 us
  waiting for transfers between devices: 63.1 us -> 18.5 us
  matrix products: 27.6 us -> 0 us
  Pallas kernels: 0 us -> 25.8 us
  between operations: 14.9 us -> 0.22 us
  loops' own time: 12.1 us -> 0 us
  starting transfers between devices: 4.82 us -> 13.9 us
  other arithmetic: 4.62 us -> 0.01 us
    reduce_scatter x1 -> x0, waiting for transfers between devices: 46.6 us -> none  [per_device(): lax.psum_scatter(partial_sum, 'task', scatter_dimension=0, tiled=True)]
    dot_general x18 -> x0, matrix products: 27.6 us -> none  [the longest x16 15.3 us: advance(): jnp.einsum('gbkij,grbkj->grbi', kernel, pieces, preferred_element_type=jn...]
    pallas_call x0 -> x14, Pallas kernels: none -> 25.8 us  [the longest x4 11.9 us: kernel_blocks(): pl.pallas_call(body, out_shape=shape((end - begin, 2 * GROUP, lat * GROUP...]
    ppermute x2 -> x12, waiting for transfers between devices: 0.01 us -> 18.5 us  [the longest x5 13.3 us: sum_fields(): other = lax.ppermute(share, 'task', partners(size, bit))]
    gather x32 -> x0, local copies, waits for them, and re-layouts: 18 us -> none  [the longest x16 9.21 us: advance(): far_jitter = jnp.take(jitter_tiles, slots, axis=1)]
    all_gather x1 -> x0, waiting for transfers between devices: 16.5 us -> none  [per_device(): lax.all_gather(smoothed, 'task', axis=0, tiled=True)]
    dynamic_slice x65 -> x0, local copies, waits for them, and re-layouts: 13.1 us -> none  [the longest x16 10.6 us: apply_kernels(): blocks = lax.map(advance, jnp.arange(tiles_dev // 2, dtype=jnp.int32))]
    another operation x1 -> x0, loops' own time: 12.1 us -> none  [apply_kernels(): blocks = lax.map(advance, jnp.arange(tiles_dev // 2, dtype=jnp.int32))]
  transfers between devices with their start and end apart: 4 -> 12, of which waited for: 2 -> 4; matrix products, arithmetic and copies ran while one was open for 4% -> 0% of each run, Pallas kernels for 0% -> 32%
where the time goes in v1:
time: 61.8 us; the launch traced here: 61.6 us
  Pallas kernels  25.8 us (42%)
  waiting for transfers between devices  18.5 us (30%)
  starting transfers between devices  13.9 us (22%)
  local copies, waits for them, and re-layouts  3.17 us (5%)
    ppermute x5, waiting for transfers between devices, sum_fields(): other = lax.ppermute(share, 'task', partners(size, bit))  13.3 us
    pallas_call x4, Pallas kernels, kernel_blocks(): pl.pallas_call(body, out_shape=shape((end - begin, 2 * GROUP, lat * GROUP...  11.9 us
    pallas_call x4, Pallas kernels, mix(): pl.pallas_call(body, out_shape=shape(values.shape, jnp.float32), in_specs...  7.73 us
    ppermute x5, starting transfers between devices, sum_fields(): other = lax.ppermute(share, 'task', partners(size, bit))  6.67 us
    ppermute x1, starting transfers between devices, per_device(): from_right = lax.ppermute(left_edge, 'site', down)  5.94 us
    pallas_call x1, Pallas kernels, project(): pl.pallas_call(body, out_shape=(shape((half, width), jnp.float32), shape(...  4.02 us
    unnamed x17, local copies, waits for them, and re-layouts  3.17 us
    ppermute x1, waiting for transfers between devices, per_device(): from_left = lax.ppermute(right_edge, 'site', up)  2.92 us
  transfers between devices with their start and end apart: 12, of which 4 were waited for; matrix products, arithmetic and copies ran while one was open for 0% of the time, Pallas kernels for 32%

profile of v1, /device:TPU:0, one launch (start us, length us, event | category | flops | bytes accessed | tf_op | source)
XLA Modules:
  0.0 61.6 jit_solution(15844559492452389638)
XLA Ops:
  0.0 2.2 %copy-done = bf16[256,8192]{1,0:T(8,128)(2,1)S(1)} copy-done((bf16[256,8192]{1,0:T(8,128)(2,1)S(1)}, bf16[256,8192]{1,0:T(8,128)(2,1)}, u32[]{:S(2)}) %copy-start) | copy-done | bytes 4194328
  2.2 0.8 %copy-done.2 = bf16[256,128]{1,0:T(8,128)(2,1)S(1)} copy-done((bf16[256,128]{1,0:T(8,128)(2,1)S(1)}, bf16[256,128]{1,0:T(8,128)(2,1)}, u32[]{:S(2)}) %copy-start.2) | copy-done | bytes 65560
  3.1 4.0 %project.1 = (f32[64,8192]{1,0:T(8,128)S(1)}, bf16[64,8192]{1,0:T(8,128)(2,1)S(1)}) custom-call(s32[1]{0:T(128)} %bitcast.core_ref, bf16[256,128]{1,0:T(8,128)(2,1)S(1)} %copy-done.2, bf16[256,8192]{1,0:T(8,128)(2,1)S(1)} %copy-done), custom_call_target="tpu_custom_call" | custom-call | flops 536870912 | bytes 4194304 | tf_op jit(solution)/shard_map/project/pallas_call | solution.py:55
  7.1 0.6 collective-permute-start
  7.6 2.3 %collective-permute-done.got_ref = bf16[64,8192]{1,0:T(8,128)(2,1)S(1)} collective-permute-done((bf16[64,8192]{1,0:T(8,128)(2,1)S(1)}, bf16[64,8192]{1,0:T(8,128)(2,1)S(1)}, u32[]{:S(2)}, u32[]{:S(2)}) %collective-permute-start) | collective-permute-done | bytes 1048608 | tf_op jit(solution)/shard_map/ppermute | solution.py:305
  10.3 5.9 %collective-permute-start.1 = (bf16[80,128]{1,0:T(8,128)(2,1)S(1)}, bf16[80,128]{1,0:T(8,128)(2,1)S(1)}, u32[]{:S(2)}, u32[]{:S(2)}) collective-permute-start(bf16[80,128]{1,0:T(8,128)(2,1)S(1)} %get-tuple-element.15), channel_id=1, source_target_pairs={{4,0},{8,4},{12,8},{16,12},{20,16},{24,20},{28,24},{0,28},{5,1},{9... | collective-permute-start | bytes 61448 | tf_op jit(solution)/shard_map/ppermute | solution.py:312
  16.2 1.5 %collective-permute-start.7 = (bf16[64,2560]{1,0:T(8,128)(2,1)S(1)}, bf16[64,2560]{1,0:T(8,128)(2,1)S(1)}, u32[]{:S(2)}, u32[]{:S(2)}) collective-permute-start(bf16[64,2560]{1,0:T(8,128)(2,1)S(1)} %get-tuple-element.19.refs_2_.refs_0_), channel_id=1, source_target_pairs={{0,2},{1,3},{2,0},{3,1},{4,6},{5,7},{6,4},{7,5},{8,10},{9,11},{10,... | collective-permute-start | bytes 983048 | tf_op jit(solution)/shard_map/ppermute | solution.py:287
  18.3 1.5 %collective-permute-start.4 = (bf16[64,2048]{1,0:T(8,128)(2,1)S(1)}, bf16[64,2048]{1,0:T(8,128)(2,1)S(1)}, u32[]{:S(2)}, u32[]{:S(2)}) collective-permute-start(bf16[64,2048]{1,0:T(8,128)(2,1)S(1)} %get-tuple-element.18.refs_2_.refs_0_), channel_id=1, source_target_pairs={{0,2},{1,3},{2,0},{3,1},{4,6},{5,7},{6,4},{7,5},{8,10},{9,11},{10,... | collective-permute-start | bytes 786440 | tf_op jit(solution)/shard_map/ppermute | solution.py:287
  19.8 2.9 %collective-permute-done.2 = bf16[80,128]{1,0:T(8,128)(2,1)S(1)} collective-permute-done((bf16[80,128]{1,0:T(8,128)(2,1)S(1)}, bf16[80,128]{1,0:T(8,128)(2,1)S(1)}, u32[]{:S(2)}, u32[]{:S(2)}) %collective-permute-start.2) | collective-permute-done | bytes 20512 | tf_op jit(solution)/shard_map/ppermute | solution.py:311
  22.7 1.5 %collective-permute-start.5 = (bf16[80,128]{1,0:T(8,128)(2,1)S(1)}, bf16[80,128]{1,0:T(8,128)(2,1)S(1)}, u32[]{:S(2)}, u32[]{:S(2)}) collective-permute-start(bf16[80,128]{1,0:T(8,128)(2,1)S(1)} %broadcast_select_fusion.rest_0_.refs_4_.refs_2_), channel_id=1, source_target_pairs={{0,2},{1,3},{2,0},{3,1},{4,6},{5,7},{6,4},{7,5},{8,10},{9,11},{10,... | collective-permute-start | bytes 61448 | tf_op jit(solution)/shard_map/ppermute | solution.py:287
  24.3 3.7 %kernel_blocks.7.k_ref = bf16[20,256,256]{2,1,0:T(8,128)(2,1)S(1)} custom-call(s32[1]{0:T(128)} %bitcast.core_ref, s32[32,3]{1,0:T(8,128)S(1)} %copy.10.near_ref, f32[4]{0:T(128)S(1)} %copy-done.6, bf16[2,8192]{1,0:T(2,128)(2,1)S(1)} %copy-done.4, bf16[80,128]{1,0:T(8,128)(2,1)S(1)} %broadcast_select_fusion.rest_0_.refs_4_.refs_2_), custom_call_target="tpu_custom_call" | custom-call | flops 39321600 | bytes 2621440 | tf_op jit(solution)/shard_map/kernel_blocks/pallas_call | solution.py:174
  28.1 11.1 %collective-permute-done.5.refs_5_.refs_3_ = bf16[80,128]{1,0:T(8,128)(2,1)S(1)} collective-permute-done((bf16[80,128]{1,0:T(8,128)(2,1)S(1)}, bf16[80,128]{1,0:T(8,128)(2,1)S(1)}, u32[]{:S(2)}, u32[]{:S(2)}) %collective-permute-start.5) | collective-permute-done | bytes 20512 | tf_op jit(solution)/shard_map/ppermute | solution.py:287
  39.1 0.5 smooth.7.own_ref
  39.8 3.5 %kernel_blocks.6.k_ref = bf16[20,256,256]{2,1,0:T(8,128)(2,1)S(1)} custom-call(s32[1]{0:T(128)} %bitcast.core_ref, s32[32,3]{1,0:T(8,128)S(1)} %copy.10.near_ref, f32[4]{0:T(128)S(1)} %copy-done.6, bf16[2,8192]{1,0:T(2,128)(2,1)S(1)} %copy-done.4), custom_call_target="tpu_custom_call" | custom-call | flops 39321600 | bytes 2621440 | tf_op jit(solution)/shard_map/kernel_blocks/pallas_call | solution.py:174
  43.3 0.5 smooth.6.own_ref
  43.8 0.6 collective-permute-start.10
  44.4 2.9 %kernel_blocks.5.k_ref = bf16[16,256,256]{2,1,0:T(8,128)(2,1)S(1)} custom-call(s32[1]{0:T(128)} %bitcast.core_ref, s32[32,3]{1,0:T(8,128)S(1)} %copy.10.near_ref, f32[4]{0:T(128)S(1)} %copy-done.6, bf16[2,8192]{1,0:T(2,128)(2,1)S(1)} %copy-done.4), custom_call_target="tpu_custom_call" | custom-call | flops 31457280 | bytes 2097152 | tf_op jit(solution)/shard_map/kernel_blocks/pallas_call | solution.py:174
  47.9 1.6 %collective-permute-start.3 = (bf16[64,896]{1,0:T(8,128)(2,1)S(1)}, bf16[64,896]{1,0:T(8,128)(2,1)S(1)}, u32[]{:S(2)}, u32[]{:S(2)}) collective-permute-start(bf16[64,896]{1,0:T(8,128)(2,1)S(1)} %get-tuple-element.17.refs_0_), channel_id=1, source_target_pairs={{0,2},{1,3},{2,0},{3,1},{4,6},{5,7},{6,4},{7,5},{8,10},{9,11},{10,... | collective-permute-start | bytes 344072 | tf_op jit(solution)/shard_map/ppermute | solution.py:287
  49.5 1.7 %kernel_blocks.4.k_ref = bf16[8,256,256]{2,1,0:T(8,128)(2,1)S(1)} custom-call(s32[1]{0:T(128)} %bitcast.core_ref, s32[32,3]{1,0:T(8,128)S(1)} %copy.10.near_ref, f32[4]{0:T(128)S(1)} %copy-done.6, bf16[2,8192]{1,0:T(2,128)(2,1)S(1)} %copy-done.4, bf16[80,128]{1,0:T(8,128)(2,1)S(1)} %broadcast_select_fusion.rest_0_.refs_4_.refs_2_), custom_call_target="tpu_custom_call" | custom-call | flops 15728640 | bytes 1048576 | tf_op jit(solution)/shard_map/kernel_blocks/pallas_call | solution.py:174
  51.2 2.2 %collective-permute-done.3.refs_1_ = bf16[64,896]{1,0:T(8,128)(2,1)S(1)} collective-permute-done((bf16[64,896]{1,0:T(8,128)(2,1)S(1)}, bf16[64,896]{1,0:T(8,128)(2,1)S(1)}, u32[]{:S(2)}, u32[]{:S(2)}) %collective-permute-start.3) | collective-permute-done | bytes 114720 | tf_op jit(solution)/shard_map/ppermute | solution.py:287
  53.8 2.2 %mix.4.rest_0_ = f32[256,8192]{1,0:T(8,128)} custom-call(s32[1]{0:T(128)} %bitcast.core_ref, bf16[64,2560]{1,0:T(8,128)(2,1)S(1)} %smooth.7.own_ref, bf16[64,2560]{1,0:T(8,128)(2,1)S(1)} %collective-permute-done.11.got_ref, bf16[256,128]{1,0:T(8,128)(2,1)S(1)} %copy-done.3, f32[1,256]{1,0:T(1,128)S(1)} %bitcast.2, bf16[256,8192]{1,0:T(8,128)(2,1)S(1)} %copy-done.1), custom_call_target="tpu_custom_call" | custom-call | flops 167772160 | bytes 3932160 | tf_op jit(solution)/shard_map/mix/pallas_call | solution.py:259
  56.1 2.2 %mix.5.rest_0_ = f32[256,8192]{1,0:T(8,128)} custom-call(s32[1]{0:T(128)} %bitcast.core_ref, bf16[64,2560]{1,0:T(8,128)(2,1)S(1)} %smooth.6.own_ref, bf16[64,2560]{1,0:T(8,128)(2,1)S(1)} %collective-permute-done.10.got_ref, bf16[256,128]{1,0:T(8,128)(2,1)S(1)} %copy-done.3, f32[1,256]{1,0:T(1,128)S(1)} %bitcast.3, ...), custom_call_target="tpu_custom_call", output_to_operand_aliasing={{}: (6, {})} | custom-call | flops 167772160 | bytes 3932160 | tf_op jit(solution)/shard_map/mix/pallas_call | solution.py:259
  58.3 1.9 %mix.6.rest_0_ = f32[256,8192]{1,0:T(8,128)} custom-call(s32[1]{0:T(128)} %bitcast.core_ref, bf16[64,2048]{1,0:T(8,128)(2,1)S(1)} %smooth.5.own_ref, bf16[64,2048]{1,0:T(8,128)(2,1)S(1)} %collective-permute-done.8.got_ref, bf16[256,128]{1,0:T(8,128)(2,1)S(1)} %copy-done.3, f32[1,256]{1,0:T(1,128)S(1)} %bitcast.4, ...), custom_call_target="tpu_custom_call", output_to_operand_aliasing={{}: (6, {})} | custom-call | flops 134217728 | bytes 3145728 | tf_op jit(solution)/shard_map/mix/pallas_call | solution.py:259
  60.2 1.4 %mix.7 = f32[256,8192]{1,0:T(8,128)} custom-call(s32[1]{0:T(128)} %bitcast.core_ref, bf16[64,1024]{1,0:T(8,128)(2,1)S(1)} %smooth.4.own_ref, bf16[64,1024]{1,0:T(8,128)(2,1)S(1)} %collective-permute-done.6.got_ref, bf16[256,128]{1,0:T(8,128)(2,1)S(1)} %copy-done.3, f32[1,256]{1,0:T(1,128)S(1)} %bitcast.5, ...), custom_call_target="tpu_custom_call", output_to_operand_aliasing={{}: (6, {})} | custom-call | flops 67108864 | bytes 1572864 | tf_op jit(solution)/shard_map/mix/pallas_call | solution.py:259
  (33 shorter events, 2.0 us)
Async XLA Ops:
  0.0 24.2 %copy-start.7 = (s32[32,3]{0,1:T(4,128)S(1)}, s32[32,3]{0,1:T(4,128)}, u32[]{:S(2)}) copy-start(s32[32,3]{0,1:T(4,128)} %param.11) | copy-start | bytes 1156
  0.0 24.3 %copy-start.6 = (f32[4]{0:T(128)S(1)}, f32[4]{0:T(128)}, u32[]{:S(2)}) copy-start(f32[4]{0:T(128)} %scale_ref.7) | copy-start | bytes 52
  0.0 2.2 %copy-start = (bf16[256,8192]{1,0:T(8,128)(2,1)S(1)}, bf16[256,8192]{1,0:T(8,128)(2,1)}, u32[]{:S(2)}) copy-start(bf16[256,8192]{1,0:T(8,128)(2,1)} %v_hbm.9) | copy-start | bytes 12582916
  2.2 0.8 %copy-start.2 = (bf16[256,128]{1,0:T(8,128)(2,1)S(1)}, bf16[256,128]{1,0:T(8,128)(2,1)}, u32[]{:S(2)}) copy-start(bf16[256,128]{1,0:T(8,128)(2,1)} %f_ref.9) | copy-start | bytes 196612
  3.1 6.9 %copy-start.4 = (bf16[2,8192]{1,0:T(2,128)(2,1)S(1)}, bf16[2,8192]{1,0:T(2,128)(2,1)}, u32[]{:S(2)}) copy-start(bf16[2,8192]{1,0:T(2,128)(2,1)} %j_ref.9) | copy-start | bytes 98308
  7.1 2.8 %collective-permute-start = (bf16[64,8192]{1,0:T(8,128)(2,1)S(1)}, bf16[64,8192]{1,0:T(8,128)(2,1)S(1)}, u32[]{:S(2)}, u32[]{:S(2)}) collective-permute-start(bf16[64,8192]{1,0:T(8,128)(2,1)S(1)} %get-tuple-element.14), channel_id=1, source_target_pairs={{0,1},{1,0},{2,3},{3,2},{4,5},{5,4},{6,7},{7,6},{8,9},{9,8},{10,11... | collective-permute-start | bytes 3145736 | tf_op jit(solution)/shard_map/ppermute | solution.py:305
  10.3 9.5 %collective-permute-start.1 = (bf16[80,128]{1,0:T(8,128)(2,1)S(1)}, bf16[80,128]{1,0:T(8,128)(2,1)S(1)}, u32[]{:S(2)}, u32[]{:S(2)}) collective-permute-start(bf16[80,128]{1,0:T(8,128)(2,1)S(1)} %get-tuple-element.15), channel_id=1, source_target_pairs={{4,0},{8,4},{12,8},{16,12},{20,16},{24,20},{28,24},{0,28},{5,1},{9... | collective-permute-start | bytes 61448 | tf_op jit(solution)/shard_map/ppermute | solution.py:312
  16.2 6.5 %collective-permute-start.2 = (bf16[80,128]{1,0:T(8,128)(2,1)S(1)}, bf16[80,128]{1,0:T(8,128)(2,1)S(1)}, u32[]{:S(2)}, u32[]{:S(2)}) collective-permute-start(bf16[80,128]{1,0:T(8,128)(2,1)S(1)} %get-tuple-element.16), channel_id=1, source_target_pairs={{0,4},{4,8},{8,12},{12,16},{16,20},{20,24},{24,28},{28,0},{1,5},{5... | collective-permute-start | bytes 61448 | tf_op jit(solution)/shard_map/ppermute | solution.py:311
  16.2 27.0 %collective-permute-start.7 = (bf16[64,2560]{1,0:T(8,128)(2,1)S(1)}, bf16[64,2560]{1,0:T(8,128)(2,1)S(1)}, u32[]{:S(2)}, u32[]{:S(2)}) collective-permute-start(bf16[64,2560]{1,0:T(8,128)(2,1)S(1)} %get-tuple-element.19.refs_2_.refs_0_), channel_id=1, source_target_pairs={{0,2},{1,3},{2,0},{3,1},{4,6},{5,7},{6,4},{7,5},{8,10},{9,11},{10,... | collective-permute-start | bytes 983048 | tf_op jit(solution)/shard_map/ppermute | solution.py:287
  17.8 21.4 %collective-permute-start.9 = (bf16[64,2688]{1,0:T(8,128)(2,1)S(1)}, bf16[64,2688]{1,0:T(8,128)(2,1)S(1)}, u32[]{:S(2)}, u32[]{:S(2)}) collective-permute-start(bf16[64,2688]{1,0:T(8,128)(2,1)S(1)} %get-tuple-element.20.refs_2_.refs_0_), channel_id=1, source_target_pairs={{0,2},{1,3},{2,0},{3,1},{4,6},{5,7},{6,4},{7,5},{8,10},{9,11},{10,... | collective-permute-start | bytes 1032200 | tf_op jit(solution)/shard_map/ppermute | solution.py:287
  18.3 29.1 %collective-permute-start.4 = (bf16[64,2048]{1,0:T(8,128)(2,1)S(1)}, bf16[64,2048]{1,0:T(8,128)(2,1)S(1)}, u32[]{:S(2)}, u32[]{:S(2)}) collective-permute-start(bf16[64,2048]{1,0:T(8,128)(2,1)S(1)} %get-tuple-element.18.refs_2_.refs_0_), channel_id=1, source_target_pairs={{0,2},{1,3},{2,0},{3,1},{4,6},{5,7},{6,4},{7,5},{8,10},{9,11},{10,... | collective-permute-start | bytes 786440 | tf_op jit(solution)/shard_map/ppermute | solution.py:287
  22.7 16.4 %collective-permute-start.5 = (bf16[80,128]{1,0:T(8,128)(2,1)S(1)}, bf16[80,128]{1,0:T(8,128)(2,1)S(1)}, u32[]{:S(2)}, u32[]{:S(2)}) collective-permute-start(bf16[80,128]{1,0:T(8,128)(2,1)S(1)} %broadcast_select_fusion.rest_0_.refs_4_.refs_2_), channel_id=1, source_target_pairs={{0,2},{1,3},{2,0},{3,1},{4,6},{5,7},{6,4},{7,5},{8,10},{9,11},{10,... | collective-permute-start | bytes 61448 | tf_op jit(solution)/shard_map/ppermute | solution.py:287
  39.7 14.1 %collective-permute-start.11 = (bf16[64,2560]{1,0:T(8,128)(2,1)S(1)}, bf16[64,2560]{1,0:T(8,128)(2,1)S(1)}, u32[]{:S(2)}, u32[]{:S(2)}) collective-permute-start(bf16[64,2560]{1,0:T(8,128)(2,1)S(1)} %smooth.7.own_ref), channel_id=1, source_target_pairs={{0,1},{1,0},{2,3},{3,2},{4,5},{5,4},{6,7},{7,6},{8,9},{9,8},{10,11... | collective-permute-start | bytes 983048 | tf_op jit(solution)/shard_map/ppermute | solution.py:331
  43.8 10.0 %copy-start.1 = (bf16[256,8192]{1,0:T(8,128)(2,1)S(1)}, bf16[256,8192]{1,0:T(8,128)(2,1)}, u32[]{:S(2)}) copy-start(bf16[256,8192]{1,0:T(8,128)(2,1)} %v_hbm.9) | copy-start | bytes 12582916
  43.8 10.0 %copy-start.3 = (bf16[256,128]{1,0:T(8,128)(2,1)S(1)}, bf16[256,128]{1,0:T(8,128)(2,1)}, u32[]{:S(2)}) copy-start(bf16[256,128]{1,0:T(8,128)(2,1)} %f_ref.9) | copy-start | bytes 196612
  43.8 10.0 %copy-start.5 = (f32[256]{0:T(256)S(1)}, f32[256]{0:T(256)}, u32[]{:S(2)}) copy-start(f32[256]{0:T(256)} %param.10) | copy-start | bytes 3076
  43.8 12.2 %collective-permute-start.10 = (bf16[64,2560]{1,0:T(8,128)(2,1)S(1)}, bf16[64,2560]{1,0:T(8,128)(2,1)S(1)}, u32[]{:S(2)}, u32[]{:S(2)}) collective-permute-start(bf16[64,2560]{1,0:T(8,128)(2,1)S(1)} %smooth.6.own_ref), channel_id=1, source_target_pairs={{0,1},{1,0},{2,3},{3,2},{4,5},{5,4},{6,7},{7,6},{8,9},{9,8},{10,11... | collective-permute-start | bytes 983048 | tf_op jit(solution)/shard_map/ppermute | solution.py:331
  47.8 10.5 %collective-permute-start.8 = (bf16[64,2048]{1,0:T(8,128)(2,1)S(1)}, bf16[64,2048]{1,0:T(8,128)(2,1)S(1)}, u32[]{:S(2)}, u32[]{:S(2)}) collective-permute-start(bf16[64,2048]{1,0:T(8,128)(2,1)S(1)} %smooth.5.own_ref), channel_id=1, source_target_pairs={{0,1},{1,0},{2,3},{3,2},{4,5},{5,4},{6,7},{7,6},{8,9},{9,8},{10,11... | collective-permute-start | bytes 786440 | tf_op jit(solution)/shard_map/ppermute | solution.py:331
  47.9 5.5 %collective-permute-start.3 = (bf16[64,896]{1,0:T(8,128)(2,1)S(1)}, bf16[64,896]{1,0:T(8,128)(2,1)S(1)}, u32[]{:S(2)}, u32[]{:S(2)}) collective-permute-start(bf16[64,896]{1,0:T(8,128)(2,1)S(1)} %get-tuple-element.17.refs_0_), channel_id=1, source_target_pairs={{0,2},{1,3},{2,0},{3,1},{4,6},{5,7},{6,4},{7,5},{8,10},{9,11},{10,... | collective-permute-start | bytes 344072 | tf_op jit(solution)/shard_map/ppermute | solution.py:287
  53.7 6.5 %collective-permute-start.6 = (bf16[64,1024]{1,0:T(8,128)(2,1)S(1)}, bf16[64,1024]{1,0:T(8,128)(2,1)S(1)}, u32[]{:S(2)}, u32[]{:S(2)}) collective-permute-start(bf16[64,1024]{1,0:T(8,128)(2,1)S(1)} %smooth.4.own_ref), channel_id=1, source_target_pairs={{0,1},{1,0},{2,3},{3,2},{4,5},{5,4},{6,7},{7,6},{8,9},{9,8},{10,11... | collective-permute-start | bytes 393224 | tf_op jit(solution)/shard_map/ppermute | solution.py:331

commit v2 on v1

v2 whole, which is shorter than its diff:
```python
import jax
import jax.numpy as jnp
from jax import lax
from jax.experimental import pallas as pl
from jax.experimental.pallas import tpu as pltpu
from jax.sharding import PartitionSpec as P


SIDE = 16
GROUP = 128
HALF = GROUP // 2
REACH = 3 * SIDE
KAPPA = 3.0**-0.25
FAR_AWAY = 1024.0
STEP = 512
EDGE_ROWS = 16
MIB = 1 << 20

VM = pl.BlockSpec(memory_space=pltpu.VMEM)
SM = pl.BlockSpec(memory_space=pltpu.SMEM)
HBM = pl.BlockSpec(memory_space=pltpu.HBM)


def shape(dims, kind):
    return jax.ShapeDtypeStruct(dims, kind)


def grant(mib):
    return pltpu.CompilerParams(vmem_limit_bytes=mib * MIB)


def cost(flops, size):
    return pl.CostEstimate(flops=flops, bytes_accessed=size, transcendentals=0)


def project(values, factors, core):
    tasks, ranks = factors.shape
    half, width = ranks // 2, values.shape[1]
    steps = width // STEP

    def body(core_ref, f_hbm, v_hbm, own_ref, send_ref, v_ref, f_ref, sems):
        spans = [pl.ds(i * STEP, STEP) for i in range(steps)]
        first = pltpu.make_async_copy(f_hbm, f_ref, sems.at[steps])
        first.start()
        copies = [pltpu.make_async_copy(v_hbm.at[:, s], v_ref.at[:, s], sems.at[i]) for i, s in enumerate(spans)]
        for copy in copies:
            copy.start()
        is_first = core_ref[0] == 0
        first.wait()
        turned = f_ref[...].astype(jnp.float32).T.astype(jnp.bfloat16)
        for copy, s in zip(copies, spans):
            copy.wait()
            share = jnp.dot(turned, v_ref[:, s], preferred_element_type=jnp.float32)
            own_ref[:, s] = jnp.where(is_first, share[:half], share[half:]).astype(jnp.bfloat16)
            send_ref[:, s] = jnp.where(is_first, share[half:], share[:half]).astype(jnp.bfloat16)

    return pl.pallas_call(
        body,
        out_shape=(
            shape((half, width), jnp.bfloat16),
            shape((half, width), jnp.bfloat16),
        ),
        in_specs=[SM, HBM, HBM],
        out_specs=(VM, VM),
        scratch_shapes=[
            pltpu.VMEM(values.shape, values.dtype),
            pltpu.VMEM(factors.shape, factors.dtype),
            pltpu.SemaphoreType.DMA((steps + 1,)),
        ],
        compiler_params=grant(50),
        cost_estimate=cost(2 * tasks * ranks * width, tasks * width * 2),
        name="project",
    )(core, factors, values)


def add_cores(own, received, jitter, chunks):
    half = own.shape[0]
    edge = half + EDGE_ROWS

    def body(own_ref, got_ref, j_ref, *outs):
        for groups, out in zip(chunks, outs):
            for begin, end in runs(groups):
                s = slice(begin * GROUP, end * GROUP)
                place = groups.index(begin) * GROUP
                total = own_ref[:, s].astype(jnp.float32) + got_ref[:, s].astype(jnp.float32)
                out[:, place : place + (end - begin) * GROUP] = total.astype(jnp.bfloat16)
        for out, s in ((outs[-2], slice(0, GROUP)), (outs[-1], slice(-GROUP, None))):
            out[:half, :] = (own_ref[:, s].astype(jnp.float32) + got_ref[:, s].astype(jnp.float32)).astype(jnp.bfloat16)
            out[half:, :] = jnp.zeros((EDGE_ROWS, GROUP), jnp.bfloat16)
            out[half : half + 2, :] = j_ref[:, s]

    size = [(half, len(groups) * GROUP) for groups in chunks] + [(edge, GROUP)] * 2
    return pl.pallas_call(
        body,
        out_shape=[shape(dims, jnp.bfloat16) for dims in size],
        in_specs=[VM, VM, VM],
        out_specs=[VM] * len(size),
        compiler_params=grant(6),
        cost_estimate=cost(own.size, own.size * 8),
        name="add_cores",
    )(own, received, jitter)


def close_ring(from_left, from_right, share):
    half, width = share.shape

    def body(left_ref, right_ref, share_ref, out, offsets):
        first_half = lax.broadcasted_iota(jnp.int32, (1, GROUP), 1) < HALF
        out[:, :width] = share_ref[...]
        out[:, width:] = jnp.where(first_half, right_ref[:half, :], left_ref[:half, :])
        offsets[...] = jnp.where(first_half, right_ref[half:, :], left_ref[half:, :])

    return pl.pallas_call(
        body,
        out_shape=(shape((half, width + GROUP), share.dtype), shape((EDGE_ROWS, GROUP), share.dtype)),
        in_specs=[VM, VM, VM],
        out_specs=(VM, VM),
        compiler_params=grant(2),
        cost_estimate=cost(share.size, 4 * share.size),
        name="close_ring",
    )(from_left, from_right, share)


def kernel_blocks(jitter, edges, neighbours, scales, core, region, groups, lat):
    rows = GROUP + REACH

    def body(core_ref, near_ref, scale_ref, j_ref, *rest):
        k_ref = rest[-1]
        edge_ref = rest[0]
        lane = lax.broadcasted_iota(jnp.int32, (1, GROUP), 1)
        row, col = ((lane >> 4).astype(jnp.float32), (lane & (SIDE - 1)).astype(jnp.float32))
        corner = lax.broadcasted_iota(jnp.int32, (1, HALF), 1)
        corner_row, corner_col = ((corner >> 4).astype(jnp.float32), (corner & (SIDE - 1)).astype(jnp.float32))
        sub = lax.broadcasted_iota(jnp.int32, (8, GROUP), 0)
        low_half = lax.broadcasted_iota(jnp.int32, (8, GROUP), 1) < HALF
        first_half = lane < HALF
        masks = jnp.where((sub < 3) == low_half, 1.0, 0.0)
        ones = jnp.ones((1, GROUP + HALF), jnp.float32)
        nothing = jnp.zeros((1, GROUP), jnp.float32)
        none = jnp.zeros((8, GROUP), jnp.float32)
        betas = []
        for q in range(lat):
            scale = jnp.full((8, GROUP), scale_ref[core_ref[0] * lat + q], jnp.float32)
            betas.append((1.0 / (KAPPA * scale * scale))[:1])

        def offsets(b):
            if isinstance(b, int):
                return j_ref[:, b * GROUP : (b + 1) * GROUP].astype(jnp.float32)
            return j_ref[:, pl.ds(pl.multiple_of(b * GROUP, GROUP), GROUP)].astype(jnp.float32)

        def block(b, slot):
            here = offsets(b)
            before = edge_ref[:2, :].astype(jnp.float32) if isinstance(b, int) and b == 0 else offsets(b - 1)
            after = edge_ref[:2, :].astype(jnp.float32) if isinstance(b, int) and b == groups - 1 else offsets(b + 1)
            tile, odd = b // 2, b % 2 if isinstance(b, int) else lax.rem(b, 2)
            left_gap = jnp.where((odd == 0) & (near_ref[tile, 1] < 0), FAR_AWAY, 0.0)
            right_gap = jnp.where((odd == 1) & (near_ref[tile, 2] < 0), FAR_AWAY, 0.0)
            far, own = [], []
            for axis, base, end_base in ((0, row, corner_row), (1, col, corner_col)):
                past = pltpu.roll(jnp.broadcast_to(before[axis : axis + 1], (8, GROUP)), REACH, 1)[:1, :HALF]
                gaps = (left_gap, right_gap) if axis == 0 else (0.0, 0.0)
                past_base = end_base - 3.0 if axis == 0 else end_base
                next_base = end_base + 8.0 if axis == 0 else end_base
                far += [
                    jnp.concatenate([here[axis : axis + 1], past], axis=1),
                    jnp.concatenate([base, past_base], axis=1),
                    jnp.concatenate([nothing, jnp.full((1, HALF), gaps[0])], axis=1),
                    jnp.concatenate([here[axis : axis + 1], after[axis : axis + 1, :HALF]], axis=1),
                    jnp.concatenate([base, next_base], axis=1),
                    jnp.concatenate([nothing, jnp.full((1, HALF), gaps[1])], axis=1),
                    ones,
                    ones,
                ]
                mine = jnp.where(sub == 6, -jnp.broadcast_to(here[axis : axis + 1], (8, GROUP)), -jnp.broadcast_to(base, (8, GROUP)))
                own.append(jnp.where(sub < 6, masks, mine))
            left = jnp.concatenate(far, axis=0).T[:rows].astype(jnp.bfloat16)
            right = jnp.concatenate(
                [jnp.concatenate([own[0], none], axis=1), jnp.concatenate([none, own[1]], axis=1)], axis=0
            ).astype(jnp.bfloat16)
            away = jnp.dot(left, right, preferred_element_type=jnp.float32)
            across, sideways = away[:, :GROUP], away[:, GROUP:]
            distance = across * across + sideways * sideways
            for q in range(lat):
                u = jnp.maximum(1.0 / KAPPA - betas[q] * distance, 0.0)
                weight = (u * u * u * (4.0 * KAPPA**3 - u)).astype(jnp.bfloat16)
                s = slice(q * GROUP, (q + 1) * GROUP)
                zero = jnp.zeros((REACH, GROUP), jnp.bfloat16)
                k_ref[slot, :GROUP, s] = weight[:GROUP]
                k_ref[slot, GROUP : GROUP + REACH, s] = jnp.where(first_half, zero, weight[GROUP:])
                k_ref[slot, 2 * GROUP - REACH :, s] = jnp.where(first_half, weight[GROUP:], zero)
            k_ref[slot, GROUP + REACH : 2 * GROUP - REACH, :] = jnp.zeros((GROUP - 2 * REACH, lat * GROUP), jnp.bfloat16)

        count = 4
        for begin, end in runs(region):
            slot = region.index(begin)
            low, high = begin + (begin == 0), end - (end == groups)
            for b in range(begin, low):
                block(b, slot)
            whole = (high - low) // count

            def several(i, carry, low=low, shift=slot - begin):
                for m in range(count):
                    b = low + i * count + m
                    block(b, b + shift)
                return carry

            lax.fori_loop(0, whole, several, 0)
            for b in range(low + whole * count, end):
                block(b, slot + b - begin)

    size = len(region) * 2 * GROUP * lat * GROUP
    args = [core, neighbours, scales, jitter] + ([edges] if edges is not None else [])
    return pl.pallas_call(
        body,
        out_shape=shape((len(region), 2 * GROUP, lat * GROUP), jnp.bfloat16),
        in_specs=[SM, SM, SM] + [VM] * (len(args) - 3),
        out_specs=VM,
        compiler_params=grant(6),
        cost_estimate=cost(30 * size, 2 * size),
        name="kernel_blocks",
    )(*args)


def smooth(blocks, region, pieces, lat, rank, groups):
    half = lat * rank

    def body(k_ref, *refs):
        out = refs[-1]
        first_half = lax.broadcasted_iota(jnp.int32, (1, GROUP), 1) < HALF

        def part(group, which, rows):
            group = groups if group < 0 else group
            for n, (held, _) in enumerate(pieces):
                if group in held:
                    at = held.index(group) * GROUP
                    return refs[2 * n + which][rows, at : at + GROUP]

        for n, b in enumerate(region):
            for q in range(lat):
                rows = slice(q * rank, (q + 1) * rank)
                sides = [
                    jnp.concatenate(
                        [part(b, w, rows), jnp.where(first_half, part(b + 1, w, rows), part(b - 1, w, rows))], axis=1
                    )
                    for w in range(2)
                ]
                total = jnp.dot(
                    jnp.concatenate(sides, axis=0),
                    k_ref[n, :, q * GROUP : (q + 1) * GROUP],
                    preferred_element_type=jnp.float32,
                )
                out[rows, n * GROUP : (n + 1) * GROUP] = (total[:rank] + total[rank:]).astype(jnp.bfloat16)

    arrays = [a for _, pair in pieces for a in pair]
    count = len(region) * GROUP
    return pl.pallas_call(
        body,
        out_shape=shape((half, count), jnp.bfloat16),
        in_specs=[VM] * (1 + len(arrays)),
        out_specs=VM,
        compiler_params=grant(8),
        cost_estimate=cost(8 * half * GROUP * count, 4 * GROUP * lat * count),
        name="smooth",
    )(blocks, *arrays)


def mix(own, received, factors, nugget, values, product, core, region):
    tasks, ranks = factors.shape
    half, width = ranks // 2, len(region) * GROUP
    steps = width // STEP
    places = [region[i * (STEP // GROUP)] * GROUP for i in range(steps)]

    def body(core_ref, own_ref, got_ref, f_ref, g_ref, v_ref, *rest):
        o_hbm, o_buf, s_buf, sems = rest[-4:]
        s_buf[pl.ds(pl.multiple_of(core_ref[0] * half, half), half), :] = own_ref[...]
        s_buf[pl.ds(pl.multiple_of((1 - core_ref[0]) * half, half), half), :] = got_ref[...]
        noise = jnp.broadcast_to(g_ref[...], (8, tasks)).T[:, :1]
        copies = []
        for i, place in enumerate(places):
            s, p = slice(i * STEP, (i + 1) * STEP), slice(place, place + STEP)
            mixed = jnp.dot(f_ref[...], s_buf[:, s], preferred_element_type=jnp.float32)
            o_buf[:, s] = mixed + noise * v_ref[:, p].astype(jnp.float32)
            copies.append(pltpu.make_async_copy(o_buf.at[:, pl.ds(i * STEP, STEP)], o_hbm.at[:, pl.ds(place, STEP)], sems.at[i]))
            copies[-1].start()
        for copy in copies:
            copy.wait()

    args = [core, own, received, factors, nugget, values]
    specs = [SM, VM, VM, VM, VM, VM]
    alias = {}
    if product is not None:
        args.append(product)
        specs.append(HBM)
        alias = {6: 0}
    return pl.pallas_call(
        body,
        out_shape=shape(values.shape, jnp.float32),
        in_specs=specs,
        out_specs=HBM,
        scratch_shapes=[
            pltpu.VMEM((tasks, width), jnp.float32),
            pltpu.VMEM((ranks, width), jnp.bfloat16),
            pltpu.SemaphoreType.DMA((steps,)),
        ],
        input_output_aliases=alias,
        compiler_params=grant(10),
        cost_estimate=cost(2 * tasks * ranks * width, tasks * width * 4),
        name="mix",
    )(*args)


def runs(groups):
    found = []
    for g in groups:
        if found and found[-1][1] == g:
            found[-1][1] = g + 1
        else:
            found.append([g, g + 1])
    return found


def partners(size, bit):
    return [(i, i ^ bit) for i in range(size)]


def sum_fields(share, size):
    bit, other = 2, None
    while bit < size:
        if other is not None:
            share = (share.astype(jnp.float32) + other.astype(jnp.float32)).astype(jnp.bfloat16)
        other = lax.ppermute(share, "task", partners(size, bit))
        bit *= 2
    return share, other


def plan(groups):
    unit = STEP // GROUP
    units = groups // unit
    cuts = [unit * (1 + (units - 2) * n // 14) for n in (0, 5, 10, 14)]
    regions = [list(range(a, b)) for a, b in zip(cuts[:-1], cuts[1:])]
    regions.append(list(range(cuts[-1], groups)) + list(range(cuts[0])))
    starts = [cuts[0] - 1] + [c + 1 for c in cuts[1:]]
    chunks = [list(range(a, b)) for a, b in zip(starts[:-1], starts[1:])]
    chunks.append(list(range(starts[-1], groups)) + list(range(starts[0])))
    return regions, chunks


def steps_of(values, factors, jitter, length_scales, nugget, neighbours):
    peers, blocks = lax.axis_size("task"), lax.axis_size("site")
    ranks = factors.shape[1]
    lat = length_scales.shape[0] // 2
    rank = ranks // length_scales.shape[0]
    groups = values.shape[1] // GROUP
    core = (lax.axis_index("task") % 2).astype(jnp.int32).reshape(1)
    regions, chunks = plan(groups)
    nugget = nugget.reshape(1, -1)

    def build(n):
        edge_offsets = offsets if n == len(regions) - 1 else None
        return kernel_blocks(jitter, edge_offsets, neighbours, length_scales, core, regions[n], groups, lat)

    own, send = project(values, factors, core)
    received = lax.ppermute(send, "task", partners(peers, 1))
    *shares, left_edge, right_edge = add_cores(own, received, jitter, chunks)
    sums = []
    for share in shares[:-1]:
        sums.append(sum_fields(share, peers))
    up = [(i, (i + 1) % blocks) for i in range(blocks)]
    down = [(j, i) for i, j in up]
    from_left = lax.ppermute(right_edge, "site", up)
    from_right = lax.ppermute(left_edge, "site", down)
    last, offsets = close_ring(from_left, from_right, shares[-1])
    sums.append(sum_fields(last, peers))
    held_groups = chunks[:-1] + [chunks[-1] + [groups]]

    product = None
    for n, region in enumerate(regions):
        kernel = build(n)
        pieces = [(held_groups[n], sums[n])]
        if n > 0:
            pieces.append((held_groups[n - 1], sums[n - 1]))
        if n == len(regions) - 1:
            pieces.append((held_groups[0], sums[0]))
        smoothed = smooth(kernel, region, pieces, lat, rank, groups)
        other = lax.ppermute(smoothed, "task", partners(peers, 1))
        product = mix(smoothed, other, factors, nugget, values, product, core, region)
    return product


def solution(mesh):
    return jax.shard_map(
        steps_of,
        mesh=mesh,
        in_specs=(
            P("task", "site"),
            P("task", None),
            P(None, "site"),
            P(),
            P("task"),
            P("site", None),
        ),
        out_specs=P("task", "site"),
        check_vma=False,
    )
```

time: 61.8 us -> 52.8 us (0.85)
  waiting for transfers between devices: 18.5 us -> 12.3 us
  Pallas kernels: 25.8 us -> 23.6 us
  starting transfers between devices: 13.9 us -> 12.5 us
  local copies, waits for them, and re-layouts: 3.17 us -> 3.81 us
    ppermute x5 -> x4, waiting for transfers between devices: 13.3 us -> 8.31 us  [sum_fields(): other = lax.ppermute(share, 'task', partners(size, bit))]
    ppermute x7, starting transfers between devices: 7.27 us -> 5.71 us  [the longest x1 3.1 us: steps_of(): from_right = lax.ppermute(left_edge, 'site', down)]
    ppermute x7, waiting for transfers between devices: 5.22 us -> 4 us  [the longest x1 2.29 us: steps_of(): received = lax.ppermute(send, 'task', partners(peers, 1))]
    pallas_call x6 -> x7, Pallas kernels: 16.2 us -> 15.2 us  [the longest x4 10.6 us: kernel_blocks(): pl.pallas_call(body, out_shape=shape((len(region), 2 * GROUP, lat * GROUP...]
    pallas_call x4, Pallas kernels: 7.73 us -> 6.72 us  [mix(): pl.pallas_call(body, out_shape=shape(values.shape, jnp.float32), in_specs...]
    unnamed x17 -> x19, local copies, waits for them, and re-layouts: 3.17 us -> 3.81 us
    ppermute x5 -> x4, starting transfers between devices: 6.67 us -> 6.75 us  [sum_fields(): other = lax.ppermute(share, 'task', partners(size, bit))]
  transfers between devices with their start and end apart: 12 -> 11, of which waited for: 4 -> 6; matrix products, arithmetic and copies ran while one was open for 0% -> 1% of each run, Pallas kernels for 32% -> 34%
where the time goes in v2:
time: 52.8 us; the launch traced here: 52.5 us
  Pallas kernels  23.6 us (45%)
  starting transfers between devices  12.5 us (24%)
  waiting for transfers between devices  12.3 us (23%)
  local copies, waits for them, and re-layouts  3.81 us (7%)
    pallas_call x4, Pallas kernels, kernel_blocks(): pl.pallas_call(body, out_shape=shape((len(region), 2 * GROUP, lat * GROUP...  10.6 us
    ppermute x4, waiting for transfers between devices, sum_fields(): other = lax.ppermute(share, 'task', partners(size, bit))  8.31 us
    ppermute x4, starting transfers between devices, sum_fields(): other = lax.ppermute(share, 'task', partners(size, bit))  6.75 us
    pallas_call x4, Pallas kernels, mix(): pl.pallas_call(body, out_shape=shape(values.shape, jnp.float32), in_specs...  6.72 us
    pallas_call x1, Pallas kernels, project(): pl.pallas_call(body, out_shape=(shape((half, width), jnp.bfloat16), shape...  4.26 us
    unnamed x19, local copies, waits for them, and re-layouts  3.81 us
    ppermute x1, starting transfers between devices, steps_of(): from_right = lax.ppermute(left_edge, 'site', down)  3.1 us
    ppermute x1, waiting for transfers between devices, steps_of(): received = lax.ppermute(send, 'task', partners(peers, 1))  2.29 us
  transfers between devices with their start and end apart: 11, of which 6 were waited for; matrix products, arithmetic and copies ran while one was open for 1% of the time, Pallas kernels for 34%

profile of v2, /device:TPU:0, one launch (start us, length us, event | category | flops | bytes accessed | tf_op | source)
XLA Modules:
  0.0 52.5 jit_solution(7895349089232298510)
XLA Ops:
  0.0 0.9 %copy-done.1 = bf16[256,128]{1,0:T(8,128)(2,1)S(1)} copy-done((bf16[256,128]{1,0:T(8,128)(2,1)S(1)}, bf16[256,128]{1,0:T(8,128)(2,1)}, u32[]{:S(2)}) %copy-start.1) | copy-done | bytes 65560
  0.9 4.3 %project.1 = (bf16[64,8192]{1,0:T(8,128)(2,1)S(1)}, bf16[64,8192]{1,0:T(8,128)(2,1)S(1)}) custom-call(s32[1]{0:T(128)} %bitcast.core_ref, bf16[256,128]{1,0:T(8,128)(2,1)S(1)} %copy-done.1, bf16[256,8192]{1,0:T(8,128)(2,1)} %v_ref.7), custom_call_target="tpu_custom_call" | custom-call | flops 536870912 | bytes 4194304 | tf_op jit(solution)/shard_map/project/pallas_call | solution.py:57
  5.7 2.3 %collective-permute-done.got_ref = bf16[64,8192]{1,0:T(8,128)(2,1)S(1)} collective-permute-done((bf16[64,8192]{1,0:T(8,128)(2,1)S(1)}, bf16[64,8192]{1,0:T(8,128)(2,1)S(1)}, u32[]{:S(2)}, u32[]{:S(2)}) %collective-permute-start) | collective-permute-done | bytes 1048608 | tf_op jit(solution)/shard_map/ppermute | solution.py:363
  8.0 0.8 %copy-done.3 = bf16[2,8192]{1,0:T(2,128)(2,1)S(1)} copy-done((bf16[2,8192]{1,0:T(2,128)(2,1)S(1)}, bf16[2,8192]{1,0:T(2,128)(2,1)}, u32[]{:S(2)}) %copy-start.3) | copy-done | bytes 32792
  9.0 2.9 %collective-permute-start.5 = (bf16[64,2816]{1,0:T(8,128)(2,1)S(1)}, bf16[64,2816]{1,0:T(8,128)(2,1)S(1)}, u32[]{:S(2)}, u32[]{:S(2)}) collective-permute-start(bf16[64,2816]{1,0:T(8,128)(2,1)S(1)} %get-tuple-element.23.refs_4_.refs_2_.refs_0_), channel_id=1, source_target_pairs={{0,2},{1,3},{2,0},{3,1},{4,6},{5,7},{6,4},{7,5},{8,10},{9,11},{10,... | collective-permute-start | bytes 1081352 | tf_op jit(solution)/shard_map/ppermute | solution.py:331
  12.0 1.9 %collective-permute-start.4 = (bf16[64,2048]{1,0:T(8,128)(2,1)S(1)}, bf16[64,2048]{1,0:T(8,128)(2,1)S(1)}, u32[]{:S(2)}, u32[]{:S(2)}) collective-permute-start(bf16[64,2048]{1,0:T(8,128)(2,1)S(1)} %get-tuple-element.22.refs_2_.refs_0_), channel_id=1, source_target_pairs={{0,2},{1,3},{2,0},{3,1},{4,6},{5,7},{6,4},{7,5},{8,10},{9,11},{10,... | collective-permute-start | bytes 786440 | tf_op jit(solution)/shard_map/ppermute | solution.py:331
  13.9 0.8 %copy.10.near_ref = s32[32,3]{1,0:T(8,128)S(1)} copy(s32[32,3]{0,1:T(4,128)} %param.11) | data formatting | bytes 768 | tf_op args[5]
  14.7 0.8 %copy-done.4 = bf16[2,8192]{1,0:T(2,128)(2,1)S(1)} copy-done((bf16[2,8192]{1,0:T(2,128)(2,1)S(1)}, bf16[2,8192]{1,0:T(2,128)(2,1)}, u32[]{:S(2)}) %copy-start.4) | copy-done | bytes 32792
  16.1 3.2 %kernel_blocks.7.k_ref = bf16[20,256,256]{2,1,0:T(8,128)(2,1)S(1)} custom-call(s32[1]{0:T(128)} %bitcast.core_ref, s32[32,3]{1,0:T(8,128)S(1)} %copy.10.near_ref, f32[4]{0:T(128)S(1)} %copy-done.7, bf16[2,8192]{1,0:T(2,128)(2,1)S(1)} %copy-done.4), custom_call_target="tpu_custom_call" | custom-call | flops 39321600 | bytes 2621440 | tf_op jit(solution)/shard_map/kernel_blocks/pallas_call | solution.py:213
  19.3 1.9 %collective-permute-done.5.refs_5_.refs_3_.refs_1_ = bf16[64,2816]{1,0:T(8,128)(2,1)S(1)} collective-permute-done((bf16[64,2816]{1,0:T(8,128)(2,1)S(1)}, bf16[64,2816]{1,0:T(8,128)(2,1)S(1)}, u32[]{:S(2)}, u32[]{:S(2)}) %collective-permute-start.5) | collective-permute-done | bytes 360480 | tf_op jit(solution)/shard_map/ppermute | solution.py:331
  21.8 3.2 %kernel_blocks.6.k_ref = bf16[20,256,256]{2,1,0:T(8,128)(2,1)S(1)} custom-call(s32[1]{0:T(128)} %bitcast.core_ref, s32[32,3]{1,0:T(8,128)S(1)} %copy.10.near_ref, f32[4]{0:T(128)S(1)} %copy-done.8, bf16[2,8192]{1,0:T(2,128)(2,1)S(1)} %copy-done.5), custom_call_target="tpu_custom_call" | custom-call | flops 39321600 | bytes 2621440 | tf_op jit(solution)/shard_map/kernel_blocks/pallas_call | solution.py:213
  25.0 3.2 %collective-permute-done.7.refs_3_.refs_1_ = bf16[64,2560]{1,0:T(8,128)(2,1)S(1)} collective-permute-done((bf16[64,2560]{1,0:T(8,128)(2,1)S(1)}, bf16[64,2560]{1,0:T(8,128)(2,1)S(1)}, u32[]{:S(2)}, u32[]{:S(2)}) %collective-permute-start.7) | collective-permute-done | bytes 327712 | tf_op jit(solution)/shard_map/ppermute | solution.py:331
  28.8 2.7 %kernel_blocks.5.k_ref = bf16[16,256,256]{2,1,0:T(8,128)(2,1)S(1)} custom-call(s32[1]{0:T(128)} %bitcast.core_ref, s32[32,3]{1,0:T(8,128)S(1)} %copy.10.near_ref, f32[4]{0:T(128)S(1)} %copy-done.8, bf16[2,8192]{1,0:T(2,128)(2,1)S(1)} %copy-done.5), custom_call_target="tpu_custom_call" | custom-call | flops 31457280 | bytes 2097152 | tf_op jit(solution)/shard_map/kernel_blocks/pallas_call | solution.py:213
  31.5 1.8 %collective-permute-done.4.refs_3_.refs_1_ = bf16[64,2048]{1,0:T(8,128)(2,1)S(1)} collective-permute-done((bf16[64,2048]{1,0:T(8,128)(2,1)S(1)}, bf16[64,2048]{1,0:T(8,128)(2,1)S(1)}, u32[]{:S(2)}, u32[]{:S(2)}) %collective-permute-start.4) | collective-permute-done | bytes 262176 | tf_op jit(solution)/shard_map/ppermute | solution.py:331
  33.8 1.8 %collective-permute-start.1 = (bf16[80,128]{1,0:T(8,128)(2,1)S(1)}, bf16[80,128]{1,0:T(8,128)(2,1)S(1)}, u32[]{:S(2)}, u32[]{:S(2)}) collective-permute-start(bf16[80,128]{1,0:T(8,128)(2,1)S(1)} %get-tuple-element.17), channel_id=1, source_target_pairs={{0,4},{4,8},{8,12},{12,16},{16,20},{20,24},{24,28},{28,0},{1,5},{5... | collective-permute-start | bytes 61448 | tf_op jit(solution)/shard_map/ppermute | solution.py:370
  35.6 3.1 %collective-permute-start.2 = (bf16[80,128]{1,0:T(8,128)(2,1)S(1)}, bf16[80,128]{1,0:T(8,128)(2,1)S(1)}, u32[]{:S(2)}, u32[]{:S(2)}) collective-permute-start(bf16[80,128]{1,0:T(8,128)(2,1)S(1)} %get-tuple-element.18), channel_id=1, source_target_pairs={{4,0},{8,4},{12,8},{16,12},{20,16},{24,20},{28,24},{0,28},{5,1},{9... | collective-permute-start | bytes 61448 | tf_op jit(solution)/shard_map/ppermute | solution.py:371
  38.7 1.7 %collective-permute-done.1.left_ref = bf16[80,128]{1,0:T(8,128)(2,1)S(1)} collective-permute-done((bf16[80,128]{1,0:T(8,128)(2,1)S(1)}, bf16[80,128]{1,0:T(8,128)(2,1)S(1)}, u32[]{:S(2)}, u32[]{:S(2)}) %collective-permute-start.1) | collective-permute-done | bytes 20512 | tf_op jit(solution)/shard_map/ppermute | solution.py:370
  40.4 1.8 %collective-permute-start.3 = (bf16[64,896]{1,0:T(8,128)(2,1)S(1)}, bf16[64,896]{1,0:T(8,128)(2,1)S(1)}, u32[]{:S(2)}, u32[]{:S(2)}) collective-permute-start(bf16[64,896]{1,0:T(8,128)(2,1)S(1)} %get-tuple-element.21.refs_0_), channel_id=1, source_target_pairs={{0,2},{1,3},{2,0},{3,1},{4,6},{5,7},{6,4},{7,5},{8,10},{9,11},{10,... | collective-permute-start | bytes 344072 | tf_op jit(solution)/shard_map/ppermute | solution.py:331
  42.2 1.6 %kernel_blocks.4.k_ref = bf16[8,256,256]{2,1,0:T(8,128)(2,1)S(1)} custom-call(s32[1]{0:T(128)} %bitcast.core_ref, s32[32,3]{1,0:T(8,128)S(1)} %copy.10.near_ref, f32[4]{0:T(128)S(1)} %copy-done.8, bf16[2,8192]{1,0:T(2,128)(2,1)S(1)} %copy-done.5, bf16[16,128]{1,0:T(8,128)(2,1)S(1)} %get-tuple-element.20.rest_0_), custom_call_target="tpu_custom_call" | custom-call | flops 15728640 | bytes 1048576 | tf_op jit(solution)/shard_map/kernel_blocks/pallas_call | solution.py:213
  43.8 1.5 %collective-permute-done.3.refs_1_ = bf16[64,896]{1,0:T(8,128)(2,1)S(1)} collective-permute-done((bf16[64,896]{1,0:T(8,128)(2,1)S(1)}, bf16[64,896]{1,0:T(8,128)(2,1)S(1)}, u32[]{:S(2)}, u32[]{:S(2)}) %collective-permute-start.3) | collective-permute-done | bytes 114720 | tf_op jit(solution)/shard_map/ppermute | solution.py:331
  45.7 1.9 %mix.4.rest_0_ = f32[256,8192]{1,0:T(8,128)} custom-call(s32[1]{0:T(128)} %bitcast.core_ref, bf16[64,2560]{1,0:T(8,128)(2,1)S(1)} %smooth.7.own_ref, bf16[64,2560]{1,0:T(8,128)(2,1)S(1)} %collective-permute-done.10.got_ref, bf16[256,128]{1,0:T(8,128)(2,1)S(1)} %copy-done.2, f32[1,256]{1,0:T(1,128)S(1)} %bitcast.2, bf16[256,8192]{1,0:T(8,128)(2,1)S(1)} %copy-done), custom_call_target="tpu_custom_call" | custom-call | flops 167772160 | bytes 2621440 | tf_op jit(solution)/shard_map/mix/pallas_call | solution.py:295
  47.6 1.9 %mix.5.rest_0_ = f32[256,8192]{1,0:T(8,128)} custom-call(s32[1]{0:T(128)} %bitcast.core_ref, bf16[64,2560]{1,0:T(8,128)(2,1)S(1)} %smooth.6.own_ref, bf16[64,2560]{1,0:T(8,128)(2,1)S(1)} %collective-permute-done.9.got_ref, bf16[256,128]{1,0:T(8,128)(2,1)S(1)} %copy-done.2, f32[1,256]{1,0:T(1,128)S(1)} %bitcast.3, ...), custom_call_target="tpu_custom_call", output_to_operand_aliasing={{}: (6, {})} | custom-call | flops 167772160 | bytes 2621440 | tf_op jit(solution)/shard_map/mix/pallas_call | solution.py:295
  49.5 1.7 %mix.6.rest_0_ = f32[256,8192]{1,0:T(8,128)} custom-call(s32[1]{0:T(128)} %bitcast.core_ref, bf16[64,2048]{1,0:T(8,128)(2,1)S(1)} %smooth.5.own_ref, bf16[64,2048]{1,0:T(8,128)(2,1)S(1)} %collective-permute-done.8.got_ref, bf16[256,128]{1,0:T(8,128)(2,1)S(1)} %copy-done.2, f32[1,256]{1,0:T(1,128)S(1)} %bitcast.4, ...), custom_call_target="tpu_custom_call", output_to_operand_aliasing={{}: (6, {})} | custom-call | flops 134217728 | bytes 2097152 | tf_op jit(solution)/shard_map/mix/pallas_call | solution.py:295
  51.2 1.3 %mix.7 = f32[256,8192]{1,0:T(8,128)} custom-call(s32[1]{0:T(128)} %bitcast.core_ref, bf16[64,1024]{1,0:T(8,128)(2,1)S(1)} %smooth.4.own_ref, bf16[64,1024]{1,0:T(8,128)(2,1)S(1)} %collective-permute-done.6.got_ref, bf16[256,128]{1,0:T(8,128)(2,1)S(1)} %copy-done.2, f32[1,256]{1,0:T(1,128)S(1)} %bitcast.5, ...), custom_call_target="tpu_custom_call", output_to_operand_aliasing={{}: (6, {})} | custom-call | flops 67108864 | bytes 1048576 | tf_op jit(solution)/shard_map/mix/pallas_call | solution.py:295
  (32 shorter events, 3.6 us)
Async XLA Ops:
  0.0 21.8 %copy-start.8 = (f32[4]{0:T(128)S(1)}, f32[4]{0:T(128)}, u32[]{:S(2)}) copy-start(f32[4]{0:T(128)} %scale_ref.7) | copy-start | bytes 52
  0.0 0.9 %copy-start.1 = (bf16[256,128]{1,0:T(8,128)(2,1)S(1)}, bf16[256,128]{1,0:T(8,128)(2,1)}, u32[]{:S(2)}) copy-start(bf16[256,128]{1,0:T(8,128)(2,1)} %f_ref.7) | copy-start | bytes 196612
  0.9 21.0 %copy-start.5 = (bf16[2,8192]{1,0:T(2,128)(2,1)S(1)}, bf16[2,8192]{1,0:T(2,128)(2,1)}, u32[]{:S(2)}) copy-start(bf16[2,8192]{1,0:T(2,128)(2,1)} %j_ref.9) | copy-start | bytes 98308
  5.1 2.8 %collective-permute-start = (bf16[64,8192]{1,0:T(8,128)(2,1)S(1)}, bf16[64,8192]{1,0:T(8,128)(2,1)S(1)}, u32[]{:S(2)}, u32[]{:S(2)}) collective-permute-start(bf16[64,8192]{1,0:T(8,128)(2,1)S(1)} %get-tuple-element.16), channel_id=1, source_target_pairs={{0,1},{1,0},{2,3},{3,2},{4,5},{5,4},{6,7},{7,6},{8,9},{9,8},{10,11... | collective-permute-start | bytes 3145736 | tf_op jit(solution)/shard_map/ppermute | solution.py:363
  8.0 0.8 %copy-start.3 = (bf16[2,8192]{1,0:T(2,128)(2,1)S(1)}, bf16[2,8192]{1,0:T(2,128)(2,1)}, u32[]{:S(2)}) copy-start(bf16[2,8192]{1,0:T(2,128)(2,1)} %j_ref.9) | copy-start | bytes 98308
  9.0 12.2 %collective-permute-start.5 = (bf16[64,2816]{1,0:T(8,128)(2,1)S(1)}, bf16[64,2816]{1,0:T(8,128)(2,1)S(1)}, u32[]{:S(2)}, u32[]{:S(2)}) collective-permute-start(bf16[64,2816]{1,0:T(8,128)(2,1)S(1)} %get-tuple-element.23.refs_4_.refs_2_.refs_0_), channel_id=1, source_target_pairs={{0,2},{1,3},{2,0},{3,1},{4,6},{5,7},{6,4},{7,5},{8,10},{9,11},{10,... | collective-permute-start | bytes 1081352 | tf_op jit(solution)/shard_map/ppermute | solution.py:331
  11.9 16.3 %collective-permute-start.7 = (bf16[64,2560]{1,0:T(8,128)(2,1)S(1)}, bf16[64,2560]{1,0:T(8,128)(2,1)S(1)}, u32[]{:S(2)}, u32[]{:S(2)}) collective-permute-start(bf16[64,2560]{1,0:T(8,128)(2,1)S(1)} %get-tuple-element.24.refs_2_.refs_0_), channel_id=1, source_target_pairs={{0,2},{1,3},{2,0},{3,1},{4,6},{5,7},{6,4},{7,5},{8,10},{9,11},{10,... | collective-permute-start | bytes 983048 | tf_op jit(solution)/shard_map/ppermute | solution.py:331
  12.0 21.3 %collective-permute-start.4 = (bf16[64,2048]{1,0:T(8,128)(2,1)S(1)}, bf16[64,2048]{1,0:T(8,128)(2,1)S(1)}, u32[]{:S(2)}, u32[]{:S(2)}) collective-permute-start(bf16[64,2048]{1,0:T(8,128)(2,1)S(1)} %get-tuple-element.22.refs_2_.refs_0_), channel_id=1, source_target_pairs={{0,2},{1,3},{2,0},{3,1},{4,6},{5,7},{6,4},{7,5},{8,10},{9,11},{10,... | collective-permute-start | bytes 786440 | tf_op jit(solution)/shard_map/ppermute | solution.py:331
  14.7 0.8 %copy-start.4 = (bf16[2,8192]{1,0:T(2,128)(2,1)S(1)}, bf16[2,8192]{1,0:T(2,128)(2,1)}, u32[]{:S(2)}) copy-start(bf16[2,8192]{1,0:T(2,128)(2,1)} %j_ref.9) | copy-start | bytes 98308
  15.5 0.7 %copy-start.7 = (f32[4]{0:T(128)S(1)}, f32[4]{0:T(128)}, u32[]{:S(2)}) copy-start(f32[4]{0:T(128)} %scale_ref.7) | copy-start | bytes 52
  21.7 23.9 %copy-start = (bf16[256,8192]{1,0:T(8,128)(2,1)S(1)}, bf16[256,8192]{1,0:T(8,128)(2,1)}, u32[]{:S(2)}) copy-start(bf16[256,8192]{1,0:T(8,128)(2,1)} %v_ref.7) | copy-start | bytes 12582916
  21.7 23.9 %copy-start.2 = (bf16[256,128]{1,0:T(8,128)(2,1)S(1)}, bf16[256,128]{1,0:T(8,128)(2,1)}, u32[]{:S(2)}) copy-start(bf16[256,128]{1,0:T(8,128)(2,1)} %f_ref.7) | copy-start | bytes 196612
  21.7 23.9 %copy-start.6 = (f32[256]{0:T(256)S(1)}, f32[256]{0:T(256)}, u32[]{:S(2)}) copy-start(f32[256]{0:T(256)} %param.10) | copy-start | bytes 3076
  21.7 23.9 %collective-permute-start.10 = (bf16[64,2560]{1,0:T(8,128)(2,1)S(1)}, bf16[64,2560]{1,0:T(8,128)(2,1)S(1)}, u32[]{:S(2)}, u32[]{:S(2)}) collective-permute-start(bf16[64,2560]{1,0:T(8,128)(2,1)S(1)} %smooth.7.own_ref), channel_id=1, source_target_pairs={{0,1},{1,0},{2,3},{3,2},{4,5},{5,4},{6,7},{7,6},{8,9},{9,8},{10,11... | collective-permute-start | bytes 983048 | tf_op jit(solution)/shard_map/ppermute | solution.py:385
  28.7 18.8 %collective-permute-start.9 = (bf16[64,2560]{1,0:T(8,128)(2,1)S(1)}, bf16[64,2560]{1,0:T(8,128)(2,1)S(1)}, u32[]{:S(2)}, u32[]{:S(2)}) collective-permute-start(bf16[64,2560]{1,0:T(8,128)(2,1)S(1)} %smooth.6.own_ref), channel_id=1, source_target_pairs={{0,1},{1,0},{2,3},{3,2},{4,5},{5,4},{6,7},{7,6},{8,9},{9,8},{10,11... | collective-permute-start | bytes 983048 | tf_op jit(solution)/shard_map/ppermute | solution.py:385
  33.7 15.7 %collective-permute-start.8 = (bf16[64,2048]{1,0:T(8,128)(2,1)S(1)}, bf16[64,2048]{1,0:T(8,128)(2,1)S(1)}, u32[]{:S(2)}, u32[]{:S(2)}) collective-permute-start(bf16[64,2048]{1,0:T(8,128)(2,1)S(1)} %smooth.5.own_ref), channel_id=1, source_target_pairs={{0,1},{1,0},{2,3},{3,2},{4,5},{5,4},{6,7},{7,6},{8,9},{9,8},{10,11... | collective-permute-start | bytes 786440 | tf_op jit(solution)/shard_map/ppermute | solution.py:385
  33.8 6.6 %collective-permute-start.1 = (bf16[80,128]{1,0:T(8,128)(2,1)S(1)}, bf16[80,128]{1,0:T(8,128)(2,1)S(1)}, u32[]{:S(2)}, u32[]{:S(2)}) collective-permute-start(bf16[80,128]{1,0:T(8,128)(2,1)S(1)} %get-tuple-element.17), channel_id=1, source_target_pairs={{0,4},{4,8},{8,12},{12,16},{16,20},{20,24},{24,28},{28,0},{1,5},{5... | collective-permute-start | bytes 61448 | tf_op jit(solution)/shard_map/ppermute | solution.py:370
  35.6 4.8 %collective-permute-start.2 = (bf16[80,128]{1,0:T(8,128)(2,1)S(1)}, bf16[80,128]{1,0:T(8,128)(2,1)S(1)}, u32[]{:S(2)}, u32[]{:S(2)}) collective-permute-start(bf16[80,128]{1,0:T(8,128)(2,1)S(1)} %get-tuple-element.18), channel_id=1, source_target_pairs={{4,0},{8,4},{12,8},{16,12},{20,16},{24,20},{28,24},{0,28},{5,1},{9... | collective-permute-start | bytes 61448 | tf_op jit(solution)/shard_map/ppermute | solution.py:371
  40.4 4.9 %collective-permute-start.3 = (bf16[64,896]{1,0:T(8,128)(2,1)S(1)}, bf16[64,896]{1,0:T(8,128)(2,1)S(1)}, u32[]{:S(2)}, u32[]{:S(2)}) collective-permute-start(bf16[64,896]{1,0:T(8,128)(2,1)S(1)} %get-tuple-element.21.refs_0_), channel_id=1, source_target_pairs={{0,2},{1,3},{2,0},{3,1},{4,6},{5,7},{6,4},{7,5},{8,10},{9,11},{10,... | collective-permute-start | bytes 344072 | tf_op jit(solution)/shard_map/ppermute | solution.py:331
  45.6 5.6 %collective-permute-start.6 = (bf16[64,1024]{1,0:T(8,128)(2,1)S(1)}, bf16[64,1024]{1,0:T(8,128)(2,1)S(1)}, u32[]{:S(2)}, u32[]{:S(2)}) collective-permute-start(bf16[64,1024]{1,0:T(8,128)(2,1)S(1)} %smooth.4.own_ref), channel_id=1, source_target_pairs={{0,1},{1,0},{2,3},{3,2},{4,5},{5,4},{6,7},{7,6},{8,9},{9,8},{10,11... | collective-permute-start | bytes 393224 | tf_op jit(solution)/shard_map/ppermute | solution.py:385

commit v3 on v2

v3 whole, which is shorter than its diff:
```python
import jax
import jax.numpy as jnp
from jax import lax
from jax.experimental import pallas as pl
from jax.experimental.pallas import tpu as pltpu
from jax.sharding import PartitionSpec as P


SIDE = 16
GROUP = 128
HALF = GROUP // 2
REACH = 3 * SIDE
KAPPA = 3.0**-0.25
FAR_AWAY = 1024.0
STEP = 512
EDGE_ROWS = 16
MIB = 1 << 20
CUTS = (5, 11)
ROOMS = (10, 14)

VM = pl.BlockSpec(memory_space=pltpu.VMEM)
HBM = pl.BlockSpec(memory_space=pltpu.HBM)


def shape(dims, kind):
    return jax.ShapeDtypeStruct(dims, kind)


def in_hbm(x):
    return pltpu.with_memory_space_constraint(x, pltpu.HBM)


def grant(mib):
    return pltpu.CompilerParams(vmem_limit_bytes=mib * MIB)


def cost(flops, size):
    return pl.CostEstimate(flops=flops, bytes_accessed=size, transcendentals=0)


def tiles(groups):
    found, place = [], 0
    for begin, end in runs(groups):
        for at in range(begin * GROUP, end * GROUP, STEP):
            size = min(STEP, end * GROUP - at)
            found.append((at, place, size))
            place += size
    return found


def project(values, factors, groups, small=None, room=50):
    tasks, ranks = factors.shape
    half, width = ranks // 2, len(groups) * GROUP
    cuts = tiles(groups)

    def body(*refs):
        count = 2 + (3 if small else 0)
        f_hbm, v_hbm = refs[:2]
        own_ref, send_ref = refs[count : count + 2]
        v_ref, f_ref, sems = refs[-3:]
        first = pltpu.make_async_copy(f_hbm, f_ref, sems.at[len(cuts)])
        first.start()
        copies = [
            pltpu.make_async_copy(v_hbm.at[:, pl.ds(at, size)], v_ref.at[:, pl.ds(place, size)], sems.at[i])
            for i, (at, place, size) in enumerate(cuts)
        ]
        for copy in copies:
            copy.start()
        core = lax.rem(lax.axis_index("task"), 2)
        if small:
            j_hbm, n_hbm, s_hbm = refs[2:5]
            j_out, gap_out, beta_out, n_ref, s_ref, extra = refs[count + 2 : count + 8]
            others = [
                pltpu.make_async_copy(x, y, extra.at[i])
                for i, (x, y) in enumerate(((j_hbm, j_out), (n_hbm, n_ref), (s_hbm, s_ref)))
            ]
            for copy in others:
                copy.start()
        first.wait()
        turned = f_ref[...].astype(jnp.float32).T.astype(jnp.bfloat16)
        for copy, (_, place, size) in zip(copies, cuts):
            copy.wait()
            s = slice(place, place + size)
            share = jnp.dot(turned, v_ref[:, s], preferred_element_type=jnp.float32)
            own_ref[:, s] = jnp.where(core == 0, share[:half], share[half:])
            send_ref[:, s] = jnp.where(core == 0, share[half:], share[:half]).astype(jnp.bfloat16)
        if small:
            for copy in others:
                copy.wait()
            owner = n_ref.shape[1]
            lane = lax.broadcasted_iota(jnp.int32, (owner, GROUP), 1)
            for parity in range(2):
                cut = jnp.where(n_ref[parity + 1 : parity + 2, :] < 0, FAR_AWAY, 0.0)
                column = jnp.broadcast_to(cut, (8, owner)).T[:, :1]
                gap_out[parity] = jnp.where((lane < HALF) == (parity == 0), jnp.broadcast_to(column, (owner, GROUP)), 0.0)
            count_q = s_ref.shape[1]
            lat = count_q // 2
            scale = s_ref[...]
            which = lax.broadcasted_iota(jnp.int32, (1, count_q), 1)
            beta = 1.0 / (KAPPA * scale * scale)
            for q in range(lat):
                value = jnp.sum(jnp.where(which == core * lat + q, beta, 0.0), axis=1, keepdims=True)
                beta_out[8 * q : 8 * q + 8, :] = jnp.broadcast_to(value, (8, GROUP))

    out = [shape((half, width), jnp.float32), shape((half, width), jnp.bfloat16)]
    scratch = []
    if small:
        offsets, near, scales = small
        lat = scales.shape[1] // 2
        out += [
            shape(offsets.shape, offsets.dtype),
            shape((2, near.shape[1], GROUP), jnp.float32),
            shape((8 * lat, GROUP), jnp.float32),
        ]
        scratch = [pltpu.VMEM(near.shape, near.dtype), pltpu.VMEM(scales.shape, scales.dtype), pltpu.SemaphoreType.DMA((3,))]
    args = [in_hbm(x) for x in (factors, values, *(small or ()))]
    return pl.pallas_call(
        body,
        out_shape=out,
        in_specs=[HBM] * len(args),
        out_specs=[VM] * len(out),
        scratch_shapes=scratch
        + [
            pltpu.VMEM((tasks, width), values.dtype),
            pltpu.VMEM(factors.shape, factors.dtype),
            pltpu.SemaphoreType.DMA((len(cuts) + 1,)),
        ],
        compiler_params=pltpu.CompilerParams(vmem_limit_bytes=int(room * MIB)),
        cost_estimate=cost(2 * tasks * ranks * width, tasks * width * 2),
        name="project",
    )(*args)


def add_cores(own, received, held, chunks, offsets=None):
    half = own.shape[0]
    edge = half + EDGE_ROWS

    def body(own_ref, got_ref, *refs):
        outs = refs[(0 if offsets is None else 1) :]

        def total(begin, end):
            s = slice(held.index(begin) * GROUP, held.index(end - 1) * GROUP + GROUP)
            return (own_ref[:, s] + got_ref[:, s].astype(jnp.float32)).astype(jnp.bfloat16)

        for groups, out in zip(chunks, outs):
            for begin, end in runs(groups):
                place = groups.index(begin) * GROUP
                out[:, place : place + (end - begin) * GROUP] = total(begin, end)
        if offsets is not None:
            last = offsets.shape[1] // GROUP - 1
            for out, g in ((outs[-2], 0), (outs[-1], last)):
                out[:half, :] = total(g, g + 1)
                out[half:, :] = jnp.zeros((EDGE_ROWS, GROUP), jnp.bfloat16)
                out[half : half + 2, :] = refs[0][:, g * GROUP : (g + 1) * GROUP]

    size = [(half, len(groups) * GROUP) for groups in chunks]
    args = [own, received]
    if offsets is not None:
        size += [(edge, GROUP)] * 2
        args.append(offsets)
    return pl.pallas_call(
        body,
        out_shape=[shape(dims, jnp.bfloat16) for dims in size],
        in_specs=[VM] * len(args),
        out_specs=[VM] * len(size),
        compiler_params=grant(6),
        cost_estimate=cost(own.size, own.size * 6),
        name="add_cores",
    )(*args)


def close_ring(from_left, from_right, share):
    half, width = share.shape

    def body(left_ref, right_ref, share_ref, out, offsets):
        first_half = lax.broadcasted_iota(jnp.int32, (1, GROUP), 1) < HALF
        out[:, :width] = share_ref[...]
        out[:, width:] = jnp.where(first_half, right_ref[:half, :], left_ref[:half, :])
        offsets[...] = jnp.where(first_half, right_ref[half:, :], left_ref[half:, :])

    return pl.pallas_call(
        body,
        out_shape=(shape((half, width + GROUP), share.dtype), shape((EDGE_ROWS, GROUP), share.dtype)),
        in_specs=[VM, VM, VM],
        out_specs=(VM, VM),
        compiler_params=grant(2),
        cost_estimate=cost(share.size, 4 * share.size),
        name="close_ring",
    )(from_left, from_right, share)


def kernel_blocks(offsets, gaps, betas, edges, region, groups):
    lat = betas.shape[0] // 8
    rows = GROUP + REACH
    wide = 2 * GROUP

    def body(j_ref, gap_ref, beta_ref, *rest):
        k_ref = rest[-1]
        edge_ref = rest[0]
        sub = lax.broadcasted_iota(jnp.int32, (8, wide), 0)
        lane = lax.broadcasted_iota(jnp.int32, (8, wide), 1)
        row, col = ((lane >> 4).astype(jnp.float32), (lane & (SIDE - 1)).astype(jnp.float32))
        corner = lane >= GROUP
        past_row = jnp.where(corner, row - 11.0, row)
        zero = jnp.zeros_like(row)
        far_base = (
            jnp.where(sub == 1, past_row, jnp.where(sub == 4, row, jnp.where(sub >= 6, 1.0, zero))),
            jnp.where((sub == 1) | (sub == 4), col, jnp.where(sub >= 6, 1.0, zero)),
        )
        sub_1, lane_1 = sub[:, :GROUP], lane[:, :GROUP]
        meets = jnp.where((sub_1 < 3) == (lane_1 < HALF), 1.0, 0.0)
        own_base = tuple(jnp.where(sub_1 < 6, meets, -base[:, :GROUP]) for base in (row, col))
        none = jnp.zeros((8, GROUP), jnp.float32)
        first_half = lax.broadcasted_iota(jnp.int32, (1, GROUP), 1) < HALF
        scale = [beta_ref[8 * q : 8 * q + 1, :] for q in range(lat)]

        def columns(b):
            if isinstance(b, int):
                return j_ref[:, b * GROUP : (b + 1) * GROUP].astype(jnp.float32)
            return j_ref[:, pl.ds(pl.multiple_of(b * GROUP, GROUP), GROUP)].astype(jnp.float32)

        def eight(x):
            return jnp.broadcast_to(x, (8, GROUP))

        def block(b, parity, slot):
            here = columns(b)
            before = edge_ref[:2, :].astype(jnp.float32) if isinstance(b, int) and b == 0 else columns(b - 1)
            after = edge_ref[:2, :].astype(jnp.float32) if isinstance(b, int) and b == groups - 1 else columns(b + 1)
            gap = eight(gap_ref[parity, pl.ds(b // 2, 1), :])
            far, own = [], []
            for axis in range(2):
                mine = eight(here[axis : axis + 1])
                past = pltpu.roll(eight(before[axis : axis + 1]), REACH, 1)
                coming = eight(after[axis : axis + 1])
                base = far_base[axis]
                left = jnp.where((sub_1 == 0) | (sub_1 == 3), mine, base[:, :GROUP])
                right = jnp.where(sub_1 == 0, past, jnp.where(sub_1 == 3, coming, base[:, GROUP:]))
                if axis == 0 and parity == 0:
                    right = jnp.where(sub_1 == 2, gap, right)
                if axis == 0 and parity == 1:
                    right = jnp.where(sub_1 == 5, pltpu.roll(gap, HALF, 1), right)
                far.append(jnp.concatenate([left, right], axis=1))
                own.append(jnp.where(sub_1 == 6, -mine, own_base[axis]))
            left = jnp.concatenate(far, axis=0).T[:rows].astype(jnp.bfloat16)
            right = jnp.concatenate(
                [jnp.concatenate([own[0], none], axis=1), jnp.concatenate([none, own[1]], axis=1)], axis=0
            ).astype(jnp.bfloat16)
            away = jnp.dot(left, right, preferred_element_type=jnp.float32)
            across, sideways = away[:, :GROUP], away[:, GROUP:]
            distance = across * across + sideways * sideways
            for q in range(lat):
                u = jnp.maximum(1.0 / KAPPA - scale[q] * distance, 0.0)
                weight = (u * u * u * (4.0 * KAPPA**3 - u)).astype(jnp.bfloat16)
                s = slice(q * GROUP, (q + 1) * GROUP)
                blank = jnp.zeros((REACH, GROUP), jnp.bfloat16)
                k_ref[slot, :GROUP, s] = weight[:GROUP]
                k_ref[slot, GROUP : GROUP + REACH, s] = jnp.where(first_half, blank, weight[GROUP:])
                k_ref[slot, wide - REACH :, s] = jnp.where(first_half, weight[GROUP:], blank)
            k_ref[slot, GROUP + REACH : wide - REACH, :] = jnp.zeros((GROUP - 2 * REACH, lat * GROUP), jnp.bfloat16)

        count = 8
        for begin, end in runs(region):
            slot = region.index(begin)
            low, high = begin + (begin == 0), end - (end == groups)
            low += low % 2
            for b in range(begin, low):
                block(b, b % 2, slot + b - begin)
            whole = (high - low) // count

            def several(i, carry, low=low, shift=slot - begin):
                for m in range(count):
                    b = low + i * count + m
                    block(b, m % 2, b + shift)
                return carry

            if whole > 1:
                lax.fori_loop(0, whole, several, 0)
            else:
                whole = 0
            for b in range(low + whole * count, end):
                block(b, b % 2, slot + b - begin)

    size = len(region) * wide * lat * GROUP
    args = [offsets, gaps, betas] + ([edges] if edges is not None else [])
    return pl.pallas_call(
        body,
        out_shape=shape((len(region), wide, lat * GROUP), jnp.bfloat16),
        in_specs=[VM] * len(args),
        out_specs=VM,
        compiler_params=grant(6),
        cost_estimate=cost(30 * size, 2 * size),
        name="kernel_blocks",
    )(*args)


def smooth(blocks, region, pieces, lat, rank, groups):
    half = lat * rank

    def body(k_ref, *refs):
        out = refs[-1]
        first_half = lax.broadcasted_iota(jnp.int32, (1, GROUP), 1) < HALF

        def part(group, which, rows):
            group = groups if group < 0 else group
            for n, (held, _) in enumerate(pieces):
                if group in held:
                    at = held.index(group) * GROUP
                    return refs[2 * n + which][rows, at : at + GROUP]

        for n, b in enumerate(region):
            for q in range(lat):
                rows = slice(q * rank, (q + 1) * rank)
                sides = [
                    jnp.concatenate(
                        [part(b, w, rows), jnp.where(first_half, part(b + 1, w, rows), part(b - 1, w, rows))], axis=1
                    )
                    for w in range(2)
                ]
                total = jnp.dot(
                    jnp.concatenate(sides, axis=0),
                    k_ref[n, :, q * GROUP : (q + 1) * GROUP],
                    preferred_element_type=jnp.float32,
                )
                out[rows, n * GROUP : (n + 1) * GROUP] = (total[:rank] + total[rank:]).astype(jnp.bfloat16)

    arrays = [a for _, pair in pieces for a in pair]
    count = len(region) * GROUP
    return pl.pallas_call(
        body,
        out_shape=shape((half, count), jnp.bfloat16),
        in_specs=[VM] * (1 + len(arrays)),
        out_specs=VM,
        compiler_params=grant(8),
        cost_estimate=cost(8 * half * GROUP * count, 4 * GROUP * lat * count),
        name="smooth",
    )(blocks, *arrays)


def mix(own, received, factors, nugget, values, product, region):
    tasks, ranks = factors.shape
    half, width = ranks // 2, len(region) * GROUP
    steps = width // STEP
    places = [region[i * (STEP // GROUP)] * GROUP for i in range(steps)]

    def body(own_ref, got_ref, f_ref, g_ref, v_ref, *rest):
        o_hbm, o_buf, s_buf, sems = rest[-4:]
        core = lax.rem(lax.axis_index("task"), 2)
        s_buf[pl.ds(pl.multiple_of(core * half, half), half), :] = own_ref[...]
        s_buf[pl.ds(pl.multiple_of((1 - core) * half, half), half), :] = got_ref[...]
        noise = jnp.broadcast_to(g_ref[...], (8, tasks)).T[:, :1]
        copies = []
        for i, place in enumerate(places):
            s, p = slice(i * STEP, (i + 1) * STEP), slice(place, place + STEP)
            mixed = jnp.dot(f_ref[...], s_buf[:, s], preferred_element_type=jnp.float32)
            o_buf[:, s] = mixed + noise * v_ref[:, p].astype(jnp.float32)
            copies.append(pltpu.make_async_copy(o_buf.at[:, pl.ds(i * STEP, STEP)], o_hbm.at[:, pl.ds(place, STEP)], sems.at[i]))
            copies[-1].start()
        for copy in copies:
            copy.wait()

    args = [own, received, factors, nugget, values]
    specs = [VM, VM, VM, VM, VM]
    alias = {}
    if product is not None:
        args.append(product)
        specs.append(HBM)
        alias = {5: 0}
    return pl.pallas_call(
        body,
        out_shape=shape(values.shape, jnp.float32),
        in_specs=specs,
        out_specs=HBM,
        scratch_shapes=[
            pltpu.VMEM((tasks, width), jnp.float32),
            pltpu.VMEM((ranks, width), jnp.bfloat16),
            pltpu.SemaphoreType.DMA((steps,)),
        ],
        input_output_aliases=alias,
        compiler_params=grant(10),
        cost_estimate=cost(2 * tasks * ranks * width, tasks * width * 4),
        name="mix",
    )(*args)


def runs(groups):
    found = []
    for g in groups:
        if found and found[-1][1] == g:
            found[-1][1] = g + 1
        else:
            found.append([g, g + 1])
    return found


def partners(size, bit):
    return [(i, i ^ bit) for i in range(size)]


def sum_fields(share, size):
    bit, other = 2, None
    while bit < size:
        if other is not None:
            share = (share.astype(jnp.float32) + other.astype(jnp.float32)).astype(jnp.bfloat16)
        other = lax.ppermute(share, "task", partners(size, bit))
        bit *= 2
    return share, other


def plan(groups):
    unit = STEP // GROUP
    units = groups // unit
    cuts = [unit * (1 + (units - 2) * n // 14) for n in (0, *CUTS)]
    regions = [list(range(a, b)) for a, b in zip(cuts[:-1], cuts[1:])]
    regions.append(list(range(cuts[-1], groups)) + list(range(cuts[0])))
    starts = [cuts[0] - 1] + [c + 1 for c in cuts[1:]]
    chunks = [list(range(a, b)) for a, b in zip(starts[:-1], starts[1:])]
    chunks.append(list(range(starts[-1], groups)) + list(range(starts[0])))
    return regions, chunks


def steps_of(values, factors, jitter, length_scales, nugget, neighbours):
    peers, blocks = lax.axis_size("task"), lax.axis_size("site")
    ranks = factors.shape[1]
    lat = length_scales.shape[0] // 2
    rank = ranks // length_scales.shape[0]
    groups = values.shape[1] // GROUP
    regions, chunks = plan(groups)
    nugget = nugget.reshape(1, -1)
    small = (jitter, neighbours.T, length_scales.reshape(1, -1))

    def build(n):
        edge_offsets = outside if n == len(regions) - 1 else None
        return kernel_blocks(offsets, gaps, betas, edge_offsets, regions[n], groups)

    rest = [g for chunk in chunks[1:] for g in chunk]
    own, send, offsets, gaps, betas = project(values, factors, chunks[0], small, room=ROOMS[0])
    received = lax.ppermute(send, "task", partners(peers, 1))
    (share,) = add_cores(own, received, chunks[0], chunks[:1])
    sums = [sum_fields(share, peers)]
    own, send = project(values, factors, rest, room=ROOMS[1])
    received = lax.ppermute(send, "task", partners(peers, 1))
    *shares, left_edge, right_edge = add_cores(own, received, rest, chunks[1:], offsets)
    for share in shares[:-1]:
        sums.append(sum_fields(share, peers))
    up = [(i, (i + 1) % blocks) for i in range(blocks)]
    down = [(j, i) for i, j in up]
    from_left = lax.ppermute(right_edge, "site", up)
    from_right = lax.ppermute(left_edge, "site", down)
    last, outside = close_ring(from_left, from_right, shares[-1])
    sums.append(sum_fields(last, peers))
    held_groups = chunks[:-1] + [chunks[-1] + [groups]]

    product = None
    for n, region in enumerate(regions):
        kernel = build(n)
        pieces = [(held_groups[n], sums[n])]
        if n > 0:
            pieces.append((held_groups[n - 1], sums[n - 1]))
        if n == len(regions) - 1:
            pieces.append((held_groups[0], sums[0]))
        smoothed = smooth(kernel, region, pieces, lat, rank, groups)
        other = lax.ppermute(smoothed, "task", partners(peers, 1))
        product = mix(smoothed, other, factors, nugget, values, product, region)
    return product


def solution(mesh):
    return jax.shard_map(
        steps_of,
        mesh=mesh,
        in_specs=(
            P("task", "site"),
            P("task", None),
            P(None, "site"),
            P(),
            P("task"),
            P("site", None),
        ),
        out_specs=P("task", "site"),
        check_vma=False,
    )
```

time: 52.8 us -> 39.8 us (0.75)
  Pallas kernels: 23.6 us -> 19.5 us
  local copies, waits for them, and re-layouts: 3.81 us -> 0.02 us
  waiting for transfers between devices: 12.3 us -> 8.65 us
  starting transfers between devices: 12.5 us -> 11.3 us
    unnamed x19 -> x6, local copies, waits for them, and re-layouts: 3.81 us -> 0.02 us
    pallas_call x5, Pallas kernels: 14.9 us -> 11.9 us  [the longest x3 6.28 us: kernel_blocks(): pl.pallas_call(body, out_shape=shape((len(region), wide, lat * GROUP), jn...]
    ppermute x1 -> x2, waiting for transfers between devices: 2.29 us -> 0.01 us  [steps_of(): received = lax.ppermute(send, 'task', partners(peers, 1))]
    ppermute x4 -> x3, starting transfers between devices: 6.75 us -> 5.21 us  [sum_fields(): other = lax.ppermute(share, 'task', partners(size, bit))]
    ppermute x4 -> x3, waiting for transfers between devices: 8.31 us -> 6.88 us  [sum_fields(): other = lax.ppermute(share, 'task', partners(size, bit))]
    pallas_call x4 -> x3, Pallas kernels: 6.72 us -> 5.79 us  [mix(): pl.pallas_call(body, out_shape=shape(values.shape, jnp.float32), in_specs...]
    pallas_call x4 -> x3, Pallas kernels: 1.76 us -> 1.6 us  [smooth(): pl.pallas_call(body, out_shape=shape((half, count), jnp.bfloat16), in_spe...]
  transfers between devices with their start and end apart: 11 -> 10, of which waited for: 6 -> 3; matrix products, arithmetic and copies ran while one was open for 1% -> 0% of each run, Pallas kernels for 34% -> 36%
where the time goes in v3:
time: 39.8 us; the launch traced here: 39.6 us
  Pallas kernels  19.5 us (49%)
  starting transfers between devices  11.3 us (28%)
  waiting for transfers between devices  8.65 us (22%)
    ppermute x3, waiting for transfers between devices, sum_fields(): other = lax.ppermute(share, 'task', partners(size, bit))  6.88 us
    pallas_call x3, Pallas kernels, kernel_blocks(): pl.pallas_call(body, out_shape=shape((len(region), wide, lat * GROUP), jn...  6.28 us
    pallas_call x3, Pallas kernels, mix(): pl.pallas_call(body, out_shape=shape(values.shape, jnp.float32), in_specs...  5.79 us
    pallas_call x2, Pallas kernels, project(): pl.pallas_call(body, out_shape=out, in_specs=[HBM] * len(args), out_specs...  5.58 us
    ppermute x3, starting transfers between devices, sum_fields(): other = lax.ppermute(share, 'task', partners(size, bit))  5.21 us
    ppermute x1, starting transfers between devices, steps_of(): from_right = lax.ppermute(left_edge, 'site', down)  3.23 us
    ppermute x1, waiting for transfers between devices, steps_of(): from_left = lax.ppermute(right_edge, 'site', up)  1.76 us
    pallas_call x3, Pallas kernels, smooth(): pl.pallas_call(body, out_shape=shape((half, count), jnp.bfloat16), in_spe...  1.6 us
  transfers between devices with their start and end apart: 10, of which 3 were waited for; matrix products, arithmetic and copies ran while one was open for 0% of the time, Pallas kernels for 36%

profile of v3, /device:TPU:0, one launch (start us, length us, event | category | flops | bytes accessed | tf_op | source)
XLA Modules:
  0.0 39.6 jit_solution(14376217874035758232)
XLA Ops:
  0.0 3.2 %project.3 = (f32[64,5376]{1,0:T(8,128)S(1)}, bf16[64,5376]{1,0:T(8,128)(2,1)S(1)}) custom-call(bf16[256,128]{1,0:T(8,128)(2,1)} %f_ref.5, bf16[256,8192]{1,0:T(8,128)(2,1)} %v_ref.5), custom_call_target="tpu_custom_call" | custom-call | flops 352321536 | bytes 2752512 | tf_op jit(solution)/shard_map/project/pallas_call | solution.py:117
  3.2 0.6 %collective-permute-start = (bf16[64,5376]{1,0:T(8,128)(2,1)S(1)}, bf16[64,5376]{1,0:T(8,128)(2,1)S(1)}, u32[]{:S(2)}, u32[]{:S(2)}) collective-permute-start(bf16[64,5376]{1,0:T(8,128)(2,1)S(1)} %get-tuple-element.22), channel_id=1, source_target_pairs={{0,1},{1,0},{2,3},{3,2},{4,5},{5,4},{6,7},{7,6},{8,9},{9,8},{10,11... | collective-permute-start | bytes 2064392 | tf_op jit(solution)/shard_map/ppermute | solution.py:441
  3.8 2.4 %project.2 = (f32[64,2816]{1,0:T(8,128)S(1)}, bf16[64,2816]{1,0:T(8,128)(2,1)S(1)}, bf16[2,8192]{1,0:T(2,128)(2,1)S(1)}, f32[2,32,128]{2,1,0:T(8,128)S(1)}, f32[16,128]{1,0:T(8,128)S(1)}) custom-call(bf16[256,128]{1,0:T(8,128)(2,1)} %f_ref.5, bf16[256,8192]{1,0:T(8,128)(2,1)} %v_ref.5, bf16[2,8192]{1,0:T(2,128)(2,1)} %refs_2_.1, s32[3,32]{1,0:T(4,128)} %bitcast.6, ...), custom_call_target="tpu_custom_call" | custom-call | flops 184549376 | bytes 1441792 | tf_op jit(solution)/shard_map/project/pallas_call | solution.py:117
  6.2 0.1 collective-permute-start.5
  6.2 0.2 add_cores.2
  6.4 3.1 %collective-permute-start.4 = (bf16[64,3072]{1,0:T(8,128)(2,1)S(1)}, bf16[64,3072]{1,0:T(8,128)(2,1)S(1)}, u32[]{:S(2)}, u32[]{:S(2)}) collective-permute-start(bf16[64,3072]{1,0:T(8,128)(2,1)S(1)} %get-tuple-element.28.refs_2_.refs_0_), channel_id=1, source_target_pairs={{0,2},{1,3},{2,0},{3,1},{4,6},{5,7},{6,4},{7,5},{8,10},{9,11},{10,... | collective-permute-start | bytes 1179656 | tf_op jit(solution)/shard_map/ppermute | solution.py:404
  9.5 1.1 %collective-permute-start.6 = (bf16[64,2816]{1,0:T(8,128)(2,1)S(1)}, bf16[64,2816]{1,0:T(8,128)(2,1)S(1)}, u32[]{:S(2)}, u32[]{:S(2)}) collective-permute-start(bf16[64,2816]{1,0:T(8,128)(2,1)S(1)} %add_cores.3.refs_4_.refs_2_.refs_0_), channel_id=1, source_target_pairs={{0,2},{1,3},{2,0},{3,1},{4,6},{5,7},{6,4},{7,5},{8,10},{9,11},{10,... | collective-permute-start | bytes 1081352 | tf_op jit(solution)/shard_map/ppermute | solution.py:404
  10.7 1.5 %collective-permute-start.1 = (bf16[80,128]{1,0:T(8,128)(2,1)S(1)}, bf16[80,128]{1,0:T(8,128)(2,1)S(1)}, u32[]{:S(2)}, u32[]{:S(2)}) collective-permute-start(bf16[80,128]{1,0:T(8,128)(2,1)S(1)} %get-tuple-element.23), channel_id=1, source_target_pairs={{0,4},{4,8},{8,12},{12,16},{16,20},{20,24},{24,28},{28,0},{1,5},{5... | collective-permute-start | bytes 61448 | tf_op jit(solution)/shard_map/ppermute | solution.py:447
  12.2 3.2 %collective-permute-start.2 = (bf16[80,128]{1,0:T(8,128)(2,1)S(1)}, bf16[80,128]{1,0:T(8,128)(2,1)S(1)}, u32[]{:S(2)}, u32[]{:S(2)}) collective-permute-start(bf16[80,128]{1,0:T(8,128)(2,1)S(1)} %get-tuple-element.24), channel_id=1, source_target_pairs={{4,0},{8,4},{12,8},{16,12},{20,16},{24,20},{28,24},{0,28},{5,1},{9... | collective-permute-start | bytes 61448 | tf_op jit(solution)/shard_map/ppermute | solution.py:448
  15.4 1.8 %collective-permute-done.1.left_ref = bf16[80,128]{1,0:T(8,128)(2,1)S(1)} collective-permute-done((bf16[80,128]{1,0:T(8,128)(2,1)S(1)}, bf16[80,128]{1,0:T(8,128)(2,1)S(1)}, u32[]{:S(2)}, u32[]{:S(2)}) %collective-permute-start.1) | collective-permute-done | bytes 20512 | tf_op jit(solution)/shard_map/ppermute | solution.py:447
  17.2 1.0 %collective-permute-start.3 = (bf16[64,2432]{1,0:T(8,128)(2,1)S(1)}, bf16[64,2432]{1,0:T(8,128)(2,1)S(1)}, u32[]{:S(2)}, u32[]{:S(2)}) collective-permute-start(bf16[64,2432]{1,0:T(8,128)(2,1)S(1)} %get-tuple-element.27.refs_0_), channel_id=1, source_target_pairs={{0,2},{1,3},{2,0},{3,1},{4,6},{5,7},{6,4},{7,5},{8,10},{9,11},{10,... | collective-permute-start | bytes 933896 | tf_op jit(solution)/shard_map/ppermute | solution.py:404
  18.2 2.4 %kernel_blocks.4.k_ref = bf16[24,256,256]{2,1,0:T(8,128)(2,1)S(1)} custom-call(bf16[2,8192]{1,0:T(2,128)(2,1)S(1)} %get-tuple-element.18.refs_0_.j_ref, f32[2,32,128]{2,1,0:T(8,128)S(1)} %get-tuple-element.19.gap_ref, f32[16,128]{1,0:T(8,128)S(1)} %get-tuple-element.20.beta_ref), custom_call_target="tpu_custom_call" | custom-call | flops 47185920 | bytes 3145728 | tf_op jit(solution)/shard_map/kernel_blocks/pallas_call | solution.py:285
  20.7 6.5 %collective-permute-done.6.refs_5_.refs_3_.refs_1_ = bf16[64,2816]{1,0:T(8,128)(2,1)S(1)} collective-permute-done((bf16[64,2816]{1,0:T(8,128)(2,1)S(1)}, bf16[64,2816]{1,0:T(8,128)(2,1)S(1)}, u32[]{:S(2)}, u32[]{:S(2)}) %collective-permute-start.6) | collective-permute-done | bytes 360480 | tf_op jit(solution)/shard_map/ppermute | solution.py:404
  27.2 0.6 %smooth.4.own_ref = bf16[64,3072]{1,0:T(8,128)(2,1)S(1)} custom-call(bf16[24,256,256]{2,1,0:T(8,128)(2,1)S(1)} %kernel_blocks.4.k_ref, bf16[64,3072]{1,0:T(8,128)(2,1)S(1)} %get-tuple-element.28.refs_2_.refs_0_, bf16[64,3072]{1,0:T(8,128)(2,1)S(1)} %collective-permute-done.4.refs_3_.refs_1_, bf16[64,2816]{1,0:T(8,128)(2,1)S(1)} %add_cores.3.refs_4_.refs_2_.refs_0_, ...), custom_call_target="tpu_custom_call" | custom-call | flops 201326592 | bytes 3145728 | tf_op jit(solution)/shard_map/smooth/pallas_call | solution.py:328
  27.8 0.1 collective-permute-start.8
  27.8 2.1 %kernel_blocks.5.k_ref = bf16[20,256,256]{2,1,0:T(8,128)(2,1)S(1)} custom-call(bf16[2,8192]{1,0:T(2,128)(2,1)S(1)} %get-tuple-element.18.refs_0_.j_ref, f32[2,32,128]{2,1,0:T(8,128)S(1)} %get-tuple-element.19.gap_ref, f32[16,128]{1,0:T(8,128)S(1)} %get-tuple-element.20.beta_ref), custom_call_target="tpu_custom_call" | custom-call | flops 39321600 | bytes 2621440 | tf_op jit(solution)/shard_map/kernel_blocks/pallas_call | solution.py:285
  30.0 0.5 %smooth.5.own_ref = bf16[64,2560]{1,0:T(8,128)(2,1)S(1)} custom-call(bf16[20,256,256]{2,1,0:T(8,128)(2,1)S(1)} %kernel_blocks.5.k_ref, bf16[64,2816]{1,0:T(8,128)(2,1)S(1)} %add_cores.3.refs_4_.refs_2_.refs_0_, bf16[64,2816]{1,0:T(8,128)(2,1)S(1)} %collective-permute-done.6.refs_5_.refs_3_.refs_1_), custom_call_target="tpu_custom_call" | custom-call | flops 167772160 | bytes 2621440 | tf_op jit(solution)/shard_map/smooth/pallas_call | solution.py:328
  30.5 0.6 %collective-permute-start.9 = (bf16[64,2560]{1,0:T(8,128)(2,1)S(1)}, bf16[64,2560]{1,0:T(8,128)(2,1)S(1)}, u32[]{:S(2)}, u32[]{:S(2)}) collective-permute-start(bf16[64,2560]{1,0:T(8,128)(2,1)S(1)} %smooth.5.own_ref), channel_id=1, source_target_pairs={{0,1},{1,0},{2,3},{3,2},{4,5},{5,4},{6,7},{7,6},{8,9},{9,8},{10,11... | collective-permute-start | bytes 983048 | tf_op jit(solution)/shard_map/ppermute | solution.py:462
  31.1 1.7 %kernel_blocks.3.k_ref = bf16[20,256,256]{2,1,0:T(8,128)(2,1)S(1)} custom-call(bf16[2,8192]{1,0:T(2,128)(2,1)S(1)} %get-tuple-element.18.refs_0_.j_ref, f32[2,32,128]{2,1,0:T(8,128)S(1)} %get-tuple-element.19.gap_ref, f32[16,128]{1,0:T(8,128)S(1)} %get-tuple-element.20.beta_ref, bf16[16,128]{1,0:T(8,128)(2,1)S(1)} %get-tuple-element.26.rest_0_), custom_call_target="tpu_custom_call" | custom-call | flops 39321600 | bytes 2621440 | tf_op jit(solution)/shard_map/kernel_blocks/pallas_call | solution.py:285
  32.8 0.4 collective-permute-done.3.refs_1_
  33.2 0.5 %smooth.3.own_ref = bf16[64,2560]{1,0:T(8,128)(2,1)S(1)} custom-call(bf16[20,256,256]{2,1,0:T(8,128)(2,1)S(1)} %kernel_blocks.3.k_ref, bf16[64,2432]{1,0:T(8,128)(2,1)S(1)} %get-tuple-element.27.refs_0_, bf16[64,2432]{1,0:T(8,128)(2,1)S(1)} %collective-permute-done.3.refs_1_, bf16[64,3072]{1,0:T(8,128)(2,1)S(1)} %get-tuple-element.28.refs_2_.refs_0_, ...), custom_call_target="tpu_custom_call" | custom-call | flops 167772160 | bytes 2621440 | tf_op jit(solution)/shard_map/smooth/pallas_call | solution.py:328
  33.8 1.9 %mix.3.rest_0_ = f32[256,8192]{1,0:T(8,128)} custom-call(bf16[64,2560]{1,0:T(8,128)(2,1)S(1)} %smooth.5.own_ref, bf16[64,2560]{1,0:T(8,128)(2,1)S(1)} %collective-permute-done.9.got_ref, bf16[256,128]{1,0:T(8,128)(2,1)S(1)} %copy-done.1, f32[1,256]{1,0:T(1,128)S(1)} %bitcast.3, bf16[256,8192]{1,0:T(8,128)(2,1)S(1)} %copy-done), custom_call_target="tpu_custom_call" | custom-call | flops 167772160 | bytes 2621440 | tf_op jit(solution)/shard_map/mix/pallas_call | solution.py:368
  35.7 2.1 %mix.4.rest_0_ = f32[256,8192]{1,0:T(8,128)} custom-call(bf16[64,3072]{1,0:T(8,128)(2,1)S(1)} %smooth.4.own_ref, bf16[64,3072]{1,0:T(8,128)(2,1)S(1)} %collective-permute-done.8.got_ref, bf16[256,128]{1,0:T(8,128)(2,1)S(1)} %copy-done.1, f32[1,256]{1,0:T(1,128)S(1)} %bitcast.4, bf16[256,8192]{1,0:T(8,128)(2,1)S(1)} %copy-done, ...), custom_call_target="tpu_custom_call", output_to_operand_aliasing={{}: (5, {})} | custom-call | flops 201326592 | bytes 3145728 | tf_op jit(solution)/shard_map/mix/pallas_call | solution.py:368
  37.8 1.9 %mix.5 = f32[256,8192]{1,0:T(8,128)} custom-call(bf16[64,2560]{1,0:T(8,128)(2,1)S(1)} %smooth.3.own_ref, bf16[64,2560]{1,0:T(8,128)(2,1)S(1)} %collective-permute-done.7.got_ref, bf16[256,128]{1,0:T(8,128)(2,1)S(1)} %copy-done.1, f32[1,256]{1,0:T(1,128)S(1)} %bitcast.5, bf16[256,8192]{1,0:T(8,128)(2,1)S(1)} %copy-done, ...), custom_call_target="tpu_custom_call", output_to_operand_aliasing={{}: (5, {})} | custom-call | flops 167772160 | bytes 2621440 | tf_op jit(solution)/shard_map/mix/pallas_call | solution.py:368
  (16 shorter events, 0.2 us)
Async XLA Ops:
  3.2 3.0 %collective-permute-start = (bf16[64,5376]{1,0:T(8,128)(2,1)S(1)}, bf16[64,5376]{1,0:T(8,128)(2,1)S(1)}, u32[]{:S(2)}, u32[]{:S(2)}) collective-permute-start(bf16[64,5376]{1,0:T(8,128)(2,1)S(1)} %get-tuple-element.22), channel_id=1, source_target_pairs={{0,1},{1,0},{2,3},{3,2},{4,5},{5,4},{6,7},{7,6},{8,9},{9,8},{10,11... | collective-permute-start | bytes 2064392 | tf_op jit(solution)/shard_map/ppermute | solution.py:441
  6.2 3.3 %collective-permute-start.5 = (bf16[64,2816]{1,0:T(8,128)(2,1)S(1)}, bf16[64,2816]{1,0:T(8,128)(2,1)S(1)}, u32[]{:S(2)}, u32[]{:S(2)}) collective-permute-start(bf16[64,2816]{1,0:T(8,128)(2,1)S(1)} %get-tuple-element.30), channel_id=1, source_target_pairs={{0,1},{1,0},{2,3},{3,2},{4,5},{5,4},{6,7},{7,6},{8,9},{9,8},{10,11... | collective-permute-start | bytes 1081352 | tf_op jit(solution)/shard_map/ppermute | solution.py:437
  6.4 20.8 %collective-permute-start.4 = (bf16[64,3072]{1,0:T(8,128)(2,1)S(1)}, bf16[64,3072]{1,0:T(8,128)(2,1)S(1)}, u32[]{:S(2)}, u32[]{:S(2)}) collective-permute-start(bf16[64,3072]{1,0:T(8,128)(2,1)S(1)} %get-tuple-element.28.refs_2_.refs_0_), channel_id=1, source_target_pairs={{0,2},{1,3},{2,0},{3,1},{4,6},{5,7},{6,4},{7,5},{8,10},{9,11},{10,... | collective-permute-start | bytes 1179656 | tf_op jit(solution)/shard_map/ppermute | solution.py:404
  9.5 17.6 %collective-permute-start.6 = (bf16[64,2816]{1,0:T(8,128)(2,1)S(1)}, bf16[64,2816]{1,0:T(8,128)(2,1)S(1)}, u32[]{:S(2)}, u32[]{:S(2)}) collective-permute-start(bf16[64,2816]{1,0:T(8,128)(2,1)S(1)} %add_cores.3.refs_4_.refs_2_.refs_0_), channel_id=1, source_target_pairs={{0,2},{1,3},{2,0},{3,1},{4,6},{5,7},{6,4},{7,5},{8,10},{9,11},{10,... | collective-permute-start | bytes 1081352 | tf_op jit(solution)/shard_map/ppermute | solution.py:404
  10.7 6.5 %collective-permute-start.1 = (bf16[80,128]{1,0:T(8,128)(2,1)S(1)}, bf16[80,128]{1,0:T(8,128)(2,1)S(1)}, u32[]{:S(2)}, u32[]{:S(2)}) collective-permute-start(bf16[80,128]{1,0:T(8,128)(2,1)S(1)} %get-tuple-element.23), channel_id=1, source_target_pairs={{0,4},{4,8},{8,12},{12,16},{16,20},{20,24},{24,28},{28,0},{1,5},{5... | collective-permute-start | bytes 61448 | tf_op jit(solution)/shard_map/ppermute | solution.py:447
  12.2 5.0 %collective-permute-start.2 = (bf16[80,128]{1,0:T(8,128)(2,1)S(1)}, bf16[80,128]{1,0:T(8,128)(2,1)S(1)}, u32[]{:S(2)}, u32[]{:S(2)}) collective-permute-start(bf16[80,128]{1,0:T(8,128)(2,1)S(1)} %get-tuple-element.24), channel_id=1, source_target_pairs={{4,0},{8,4},{12,8},{16,12},{20,16},{24,20},{28,24},{0,28},{5,1},{9... | collective-permute-start | bytes 61448 | tf_op jit(solution)/shard_map/ppermute | solution.py:448
  17.2 16.0 %collective-permute-start.3 = (bf16[64,2432]{1,0:T(8,128)(2,1)S(1)}, bf16[64,2432]{1,0:T(8,128)(2,1)S(1)}, u32[]{:S(2)}, u32[]{:S(2)}) collective-permute-start(bf16[64,2432]{1,0:T(8,128)(2,1)S(1)} %get-tuple-element.27.refs_0_), channel_id=1, source_target_pairs={{0,2},{1,3},{2,0},{3,1},{4,6},{5,7},{6,4},{7,5},{8,10},{9,11},{10,... | collective-permute-start | bytes 933896 | tf_op jit(solution)/shard_map/ppermute | solution.py:404
  27.8 7.9 %collective-permute-start.8 = (bf16[64,3072]{1,0:T(8,128)(2,1)S(1)}, bf16[64,3072]{1,0:T(8,128)(2,1)S(1)}, u32[]{:S(2)}, u32[]{:S(2)}) collective-permute-start(bf16[64,3072]{1,0:T(8,128)(2,1)S(1)} %smooth.4.own_ref), channel_id=1, source_target_pairs={{0,1},{1,0},{2,3},{3,2},{4,5},{5,4},{6,7},{7,6},{8,9},{9,8},{10,11... | collective-permute-start | bytes 1179656 | tf_op jit(solution)/shard_map/ppermute | solution.py:462
  30.5 3.3 %copy-start = (bf16[256,8192]{1,0:T(8,128)(2,1)S(1)}, bf16[256,8192]{1,0:T(8,128)(2,1)}, u32[]{:S(2)}) copy-start(bf16[256,8192]{1,0:T(8,128)(2,1)} %v_ref.5) | copy-start | bytes 12582916
  30.5 3.3 %copy-start.1 = (bf16[256,128]{1,0:T(8,128)(2,1)S(1)}, bf16[256,128]{1,0:T(8,128)(2,1)}, u32[]{:S(2)}) copy-start(bf16[256,128]{1,0:T(8,128)(2,1)} %f_ref.5) | copy-start | bytes 196612
  30.5 3.3 %copy-start.2 = (f32[256]{0:T(256)S(1)}, f32[256]{0:T(256)}, u32[]{:S(2)}) copy-start(f32[256]{0:T(256)} %param.10) | copy-start | bytes 3076
  30.5 3.3 %collective-permute-start.9 = (bf16[64,2560]{1,0:T(8,128)(2,1)S(1)}, bf16[64,2560]{1,0:T(8,128)(2,1)S(1)}, u32[]{:S(2)}, u32[]{:S(2)}) collective-permute-start(bf16[64,2560]{1,0:T(8,128)(2,1)S(1)} %smooth.5.own_ref), channel_id=1, source_target_pairs={{0,1},{1,0},{2,3},{3,2},{4,5},{5,4},{6,7},{7,6},{8,9},{9,8},{10,11... | collective-permute-start | bytes 983048 | tf_op jit(solution)/shard_map/ppermute | solution.py:462
  33.7 4.1 %collective-permute-start.7 = (bf16[64,2560]{1,0:T(8,128)(2,1)S(1)}, bf16[64,2560]{1,0:T(8,128)(2,1)S(1)}, u32[]{:S(2)}, u32[]{:S(2)}) collective-permute-start(bf16[64,2560]{1,0:T(8,128)(2,1)S(1)} %smooth.3.own_ref), channel_id=1, source_target_pairs={{0,1},{1,0},{2,3},{3,2},{4,5},{5,4},{6,7},{7,6},{8,9},{9,8},{10,11... | collective-permute-start | bytes 983048 | tf_op jit(solution)/shard_map/ppermute | solution.py:462
